TPU v7x, 32 devices: a whole 2x2x4 slice. The times are simulated.
32 devices in a mesh: gy: 4 (over z), gx: 4 (over x, core), gz: 2 (over y).
Axes of the slice: x: 2, y: 2, z: 4, core: 2. Of those that a mesh axis runs over, the one named last changes fastest.
Arguments:
- velocity: float32 [3, 2, 768, 24, 512], P(None, None, 'gy', 'gx', 'gz'), may hold values from -6 to 6
- stencil: float32 [3, 768], replicated, may hold values from -2 to 2
- mode_rates: float32 [768], replicated, may hold values from 0.5 to 20
- basis: float32 [768, 768], P(('gx', 'gz')), may hold values from -0.21875 to 0.21875
Outputs:
- projected: float32 [3, 2, 768, 24, 512], P(None, None, 'gy', 'gx', 'gz')
All inputs are finite; a program needn't handle non-finite values.
Results may differ from a plain program's by a relative error of at most 0.000075.
Values sent between devices are 32-bit elements; how exact they have to be, the bound alone decides.
No kernel may reach another device: no remote copies, remote signals or barrier semaphores. Data moves between devices by JAX's collectives and lax.ppermute only.
A program may use at most 64 MiB of HBM per device.

v0:
```python
import functools

import jax
import jax.numpy as jnp
from jax import lax
from jax.experimental import pallas as pl
from jax.experimental.pallas import tpu as pltpu
from jax.sharding import PartitionSpec as P


LANES = 128
EDGE = 8


def with_halo(cells, sides, width):
    for axis, dim in sides:
        count = lax.axis_size(axis)
        ends = count - 1
        head = lax.slice_in_dim(cells, 0, width, axis=dim)
        tail = lax.slice_in_dim(cells, cells.shape[dim] - width, cells.shape[dim], axis=dim)
        cells = jnp.concatenate(
            [
                lax.ppermute(tail, axis, [(i, (i + 1) % count) for i in range(ends)]),
                cells,
                lax.ppermute(head, axis, [((i + 1) % count, i) for i in range(ends)]),
            ],
            axis=dim,
        )
    return cells


def coefficients(stencil, start, count, trailing):
    rows_part = lax.dynamic_slice_in_dim(stencil, start, count, 1)
    shape = (1, count) + (1,) * trailing
    return (rows_part[0].reshape(shape), rows_part[1].reshape(shape), rows_part[2].reshape(shape))


def slope(padded, weights):
    lower, centre, upper = weights
    return lower * padded[:, :-2] + centre * padded[:, 1:-1] + upper * padded[:, 2:]


def plain_device(velocity, stencil, mode_rates, basis):
    rows_dev = velocity.shape[2]
    kx_local = velocity.shape[3]
    span_dev = velocity.shape[4]
    rows_all = stencil.shape[1]
    groups = lax.axis_size("gy")
    flat_cols = kx_local * span_dev
    pencil_cols = flat_cols // groups
    slab_index = lax.axis_index("gy")
    stream_base = lax.axis_index("gx") * kx_local
    span_base = lax.axis_index("gz") * span_dev
    wave_x = (0.125 * (stream_base + lax.iota(jnp.int32, kx_local)).astype(jnp.float32)).reshape(
        1, kx_local, 1
    )
    wave_z = (0.05 * (span_base + lax.iota(jnp.int32, span_dev)).astype(jnp.float32)).reshape(
        1, 1, span_dev
    )
    column_ids = slab_index * pencil_cols + lax.iota(jnp.int32, pencil_cols)
    wave_px = 0.125 * (stream_base + column_ids // span_dev).astype(jnp.float32)
    wave_pz = 0.05 * (span_base + column_ids % span_dev).astype(jnp.float32)
    local_weights = coefficients(stencil, slab_index * rows_dev, rows_dev, 2)
    full_basis = lax.all_gather(basis, ("gx", "gz"), axis=0, tiled=True)
    stream = velocity[0]
    normal = velocity[1]
    span = velocity[2]
    horizontal = jnp.stack(
        [-(wave_x * stream[1]) - wave_z * span[1], wave_x * stream[0] + wave_z * span[0]]
    )
    padded = with_halo(normal, (("gy", 1),), 1)
    divergence = (horizontal + slope(padded, local_weights)).reshape(2, rows_dev, flat_cols)
    columns = lax.all_to_all(divergence, "gy", split_axis=2, concat_axis=1, tiled=True)
    modal = jnp.einsum("my,ryp->rmp", full_basis, columns, precision=lax.Precision.HIGHEST)
    scale = -1.0 / (
        mode_rates.reshape(rows_all, 1)
        + (wave_px * wave_px + wave_pz * wave_pz).reshape(1, pencil_cols)
    )
    pressure = jnp.einsum(
        "my,rmp->ryp", full_basis, modal * scale[None], precision=lax.Precision.HIGHEST
    )
    press_flat = lax.all_to_all(pressure, "gy", split_axis=1, concat_axis=2, tiled=True)
    press_slab = press_flat.reshape(2, rows_dev, kx_local, span_dev)
    press_padded = with_halo(press_slab, (("gy", 1),), 1)
    press_slope = slope(press_padded, local_weights)
    new_stream = jnp.stack([stream[0] + wave_x * press_slab[1], stream[1] - wave_x * press_slab[0]])
    new_span = jnp.stack([span[0] + wave_z * press_slab[1], span[1] - wave_z * press_slab[0]])
    new_normal = normal - press_slope
    return jnp.stack([new_stream, new_normal, new_span])


def unit_waves(place, unit, halves, gap):
    kx = lax.div(unit, halves)
    half = lax.rem(unit, halves)
    wave_x = 0.125 * (place[1] + kx).astype(jnp.float32)
    lane = lax.broadcasted_iota(jnp.int32, (gap, LANES), 1)
    wave_z = 0.05 * (place[2] + half * LANES + lane).astype(jnp.float32)
    return wave_x, wave_z


def shifted(field, before, after):
    rows = field.shape[0]
    row = lax.broadcasted_iota(jnp.int32, field.shape, 0)
    prev = jnp.where(row == 0, before, pltpu.roll(field, 1, 0))
    nxt = jnp.where(row == rows - 1, after, pltpu.roll(field, rows - 1, 0))
    return prev, nxt


def divergence_kernel(chunk, groups, halves, place, vel, weights, *outs):
    step = pl.program_id(0)
    rows = vel.shape[3]
    unit = chunk * groups + lax.rem(place[0] + step, groups)
    wave_x, wave_z = unit_waves(place, unit, halves, 1)

    def write(out):
        edges = []
        for part, sign in ((0, -1.0), (1, 1.0)):
            normal = vel[1, part, 0]
            prev, nxt = shifted(normal, 0.0, 0.0)
            out[part * rows : (part + 1) * rows, :] = (
                sign * (wave_x * vel[0, 1 - part, 0] + wave_z * vel[2, 1 - part, 0])
                + (weights[0] * prev + weights[1] * normal + weights[2] * nxt)
            )
            edges += [vel[1, part, 0, 0:1, :], vel[1, part, 0, rows - 1 : rows, :]]
        edges.append(jnp.zeros((EDGE - 4, LANES), jnp.float32))
        out[2 * rows :, :] = jnp.concatenate(edges, 0)

    for k in range(groups):
        pl.when(step == k)(functools.partial(write, outs[k]))


def split_kernel(pieces, *refs):
    sources, (high, low, high_t, low_t), full = refs[:pieces], refs[pieces:-1], refs[-1]
    at = 0
    for source in sources:
        full[at : at + source.shape[0], :] = source[...]
        at += source.shape[0]
    size = full.shape[0]
    for j in range(0, size, LANES):
        block = full[j : j + LANES, :]
        top = block.astype(jnp.bfloat16)
        high[j : j + LANES, :] = top
        low[j : j + LANES, :] = (block - top.astype(jnp.float32)).astype(jnp.bfloat16)
        block = full[:, j : j + LANES].T
        top = block.astype(jnp.bfloat16)
        high_t[j : j + LANES, :] = top
        low_t[j : j + LANES, :] = (block - top.astype(jnp.float32)).astype(jnp.bfloat16)


def three_products(high, low, values):
    top = values.astype(jnp.bfloat16)
    rest = (values - top.astype(jnp.float32)).astype(jnp.bfloat16)
    dot = functools.partial(jnp.dot, preferred_element_type=jnp.float32)
    return dot(high[...], top) + (dot(high[...], rest) + dot(low[...], top))


def solve_kernel(chunk, groups, halves, place, stencil, rates, high, low, high_t, low_t, *refs):
    blocks, outs = refs[:groups], refs[groups : 2 * groups]
    field, edge = refs[2 * groups :]
    rows = (blocks[0].shape[0] - EDGE) // 2
    rows_all = high.shape[0]
    me = place[0]
    for k in range(groups):
        source = lax.rem(me - k + groups, groups)
        base = pl.multiple_of(source * rows + EDGE, EDGE)
        for part in range(2):
            field[pl.ds(base, rows), part * LANES : (part + 1) * LANES] = blocks[k][
                part * rows : (part + 1) * rows, :
            ]
        edge[source] = blocks[k][2 * rows :, :]
    for s in range(groups - 1):
        cut = (s + 1) * rows
        for part in range(2):
            lanes = slice(part * LANES, (part + 1) * LANES)
            above = edge[s + 1, 2 * part : 2 * part + 1, :]
            below = edge[s, 2 * part + 1 : 2 * part + 2, :]
            field[EDGE + cut - 1 : EDGE + cut, lanes] += stencil[2, cut - 1] * above
            field[EDGE + cut : EDGE + cut + 1, lanes] += stencil[0, cut] * below
    modal = three_products(high, low, field[EDGE : EDGE + rows_all, :])
    wave_x, wave_z = unit_waves(place, chunk * groups + me, halves, 1)
    scale = -1.0 / (rates[...] + wave_x * wave_x + wave_z * wave_z)
    modal = jnp.concatenate([modal[:, :LANES] * scale, modal[:, LANES:] * scale], 1)
    field[EDGE : EDGE + rows_all, :] = three_products(high_t, low_t, modal)
    field[0:EDGE, :] = jnp.zeros((EDGE, 2 * LANES), jnp.float32)
    field[EDGE + rows_all :, :] = jnp.zeros((EDGE, 2 * LANES), jnp.float32)
    for k in range(groups):
        target = lax.rem(me + k, groups)
        start = pl.multiple_of(target * rows, EDGE)
        edges = []
        for part in range(2):
            lanes = slice(part * LANES, (part + 1) * LANES)
            outs[k][part * rows : (part + 1) * rows, :] = field[pl.ds(start + EDGE, rows), lanes]
            edges.append(field[pl.ds(start, EDGE), lanes][EDGE - 1 :, :])
            edges.append(field[pl.ds(start + EDGE + rows, EDGE), lanes][:1, :])
        edges.append(jnp.zeros((EDGE - 4, LANES), jnp.float32))
        outs[k][2 * rows :, :] = jnp.concatenate(edges, 0)


def project_kernel(chunk, groups, halves, place, vel, weights, *refs):
    blocks, out = refs[:groups], refs[-1]
    step = pl.program_id(0)
    rows = vel.shape[3]
    unit = chunk * groups + lax.rem(place[0] - step + groups, groups)
    wave_x, wave_z = unit_waves(place, unit, halves, 1)

    def write(block):
        for part, sign in ((0, 1.0), (1, -1.0)):
            other = block[(1 - part) * rows : (2 - part) * rows, :]
            out[0, part, 0] = vel[0, part, 0] + (sign * wave_x) * other
            out[2, part, 0] = vel[2, part, 0] + (sign * wave_z) * other
            press = block[part * rows : (part + 1) * rows, :]
            at = 2 * rows + 2 * part
            prev, nxt = shifted(press, block[at : at + 1, :], block[at + 1 : at + 2, :])
            out[1, part, 0] = vel[1, part, 0] - (
                weights[0] * prev + weights[1] * press + weights[2] * nxt
            )

    for k in range(groups):
        pl.when(step == k)(functools.partial(write, blocks[k]))


def shift_order(groups):
    return sorted(range(1, groups), key=lambda k: abs(2 * k - groups))


def gathered_rows(basis, mode_rates):
    gx, gz = lax.axis_size("gx"), lax.axis_size("gz")
    names = ("gx", "gz")
    if (gx, gz) != (4, 2):
        return [lax.all_gather(basis, names, axis=0, tiled=True)], mode_rates

    def swap(value, a, b):
        return lax.ppermute(
            value,
            names,
            [(x * gz + z, (x ^ a) * gz + (z ^ b)) for x in range(gx) for z in range(gz)],
        )

    flips = ((0, 0), (2, 0), (0, 1), (2, 1))
    pieces = [basis] + [swap(basis, *flips[i]) for i in range(1, 4)]
    pieces += [swap(piece, 1, 0) for piece in pieces]
    count = basis.shape[0]
    x, z = lax.axis_index("gx"), lax.axis_index("gz")
    order = [(a + c, b) for c in (0, 1) for a, b in flips]
    rates = jnp.concatenate(
        [
            lax.dynamic_slice_in_dim(mode_rates, ((x ^ a) * gz + (z ^ b)) * count, count, 0)
            for a, b in order
        ]
    )
    return pieces, rates


def fast_device(velocity, stencil, mode_rates, basis):
    rows, kx_local, span_dev = velocity.shape[2:]
    rows_all = stencil.shape[1]
    groups = lax.axis_size("gy")
    halves = span_dev // LANES
    chunks = kx_local * halves // groups
    me = lax.axis_index("gy")
    place = jnp.stack(
        [me, lax.axis_index("gx") * kx_local, lax.axis_index("gz") * span_dev]
    ).astype(jnp.int32)
    vel = jnp.transpose(velocity, (0, 1, 3, 2, 4))
    weights = jnp.broadcast_to(
        lax.dynamic_slice_in_dim(stencil, me * rows, rows, 1)[:, :, None], (3, rows, LANES)
    )
    block = jax.ShapeDtypeStruct((2 * rows + EDGE, LANES), jnp.float32)
    whole = pl.BlockSpec(memory_space=pltpu.VMEM)
    held = pl.BlockSpec(block.shape, lambda i, s: (0, 0))
    held_weights = pl.BlockSpec(weights.shape, lambda i, s: (0, 0, 0))
    unit_bytes = 6 * rows * LANES * 4
    params = pltpu.CompilerParams(vmem_limit_bytes=40 * 2**20)
    wide_params = pltpu.CompilerParams(vmem_limit_bytes=60 * 2**20)

    def unit_spec(chunk, sign):
        def index(i, s):
            unit = chunk * groups + lax.rem(s[0] + sign * i + groups, groups)
            return 0, 0, lax.div(unit, halves), 0, lax.rem(unit, halves)

        return pl.BlockSpec((3, 2, 1, rows, LANES), index)

    def exchange(parts):
        sent = {0: parts[0]}
        for k in shift_order(groups):
            sent[k] = lax.ppermute(parts[k], "gy", [(s, (s + k) % groups) for s in range(groups)])
        return [sent[k] for k in range(groups)]

    def diverge(chunk):
        return pl.pallas_call(
            functools.partial(divergence_kernel, chunk, groups, halves),
            grid_spec=pltpu.PrefetchScalarGridSpec(
                num_scalar_prefetch=1,
                grid=(groups,),
                in_specs=[unit_spec(chunk, 1), held_weights],
                out_specs=[held] * groups,
            ),
            out_shape=[block] * groups,
            compiler_params=wide_params,
            name="divergence",
            cost_estimate=pl.CostEstimate(
                flops=groups * unit_bytes, bytes_accessed=2 * groups * unit_bytes, transcendentals=0
            ),
        )(place, vel, weights)

    arrived = []
    for chunk in range(chunks):
        parts = diverge(chunk)
        arrived.append(exchange(parts))
    pieces, rates = gathered_rows(basis, mode_rates)
    rates = jnp.broadcast_to(rates[:, None], (rows_all, LANES))
    matrix = jax.ShapeDtypeStruct((rows_all, rows_all), jnp.bfloat16)
    splits = pl.pallas_call(
        functools.partial(split_kernel, len(pieces)),
        in_specs=[whole] * len(pieces),
        out_specs=[whole] * 4,
        out_shape=[matrix] * 4,
        scratch_shapes=[pltpu.VMEM((rows_all, rows_all), jnp.float32)],
        compiler_params=params,
        name="split",
        cost_estimate=pl.CostEstimate(
            flops=4 * rows_all**2, bytes_accessed=12 * rows_all**2, transcendentals=0
        ),
    )(*pieces)

    def solve(chunk, blocks):
        return pl.pallas_call(
            functools.partial(solve_kernel, chunk, groups, halves),
            in_specs=[pl.BlockSpec(memory_space=pltpu.SMEM)] * 2 + [whole] * (5 + groups),
            out_specs=[whole] * groups,
            out_shape=[block] * groups,
            scratch_shapes=[
                pltpu.VMEM((rows_all + 2 * EDGE, 2 * LANES), jnp.float32),
                pltpu.VMEM((groups, EDGE, LANES), jnp.float32),
            ],
            compiler_params=params,
            name="solve",
            cost_estimate=pl.CostEstimate(
                flops=12 * rows_all**2 * 2 * LANES,
                bytes_accessed=8 * rows_all**2 + 8 * block.size * groups,
                transcendentals=0,
            ),
        )(place, stencil, rates, *splits, *blocks)

    returned = []
    for chunk in range(chunks):
        parts = solve(chunk, arrived[chunk])
        returned.append(exchange(parts))
    out = None
    for chunk in range(chunks):
        carried = [] if out is None else [out]
        call = pl.pallas_call(
            functools.partial(project_kernel, chunk, groups, halves),
            grid_spec=pltpu.PrefetchScalarGridSpec(
                num_scalar_prefetch=1,
                grid=(groups,),
                in_specs=[unit_spec(chunk, -1), held_weights]
                + [held] * groups
                + [pl.BlockSpec(memory_space=pl.ANY)] * len(carried),
                out_specs=unit_spec(chunk, -1),
            ),
            out_shape=jax.ShapeDtypeStruct(vel.shape, jnp.float32),
            input_output_aliases={3 + groups: 0} if carried else {},
            compiler_params=params,
            name="project",
            cost_estimate=pl.CostEstimate(
                flops=groups * unit_bytes, bytes_accessed=3 * groups * unit_bytes, transcendentals=0
            ),
        )
        out = call(place, vel, weights, *returned[chunk], *carried)
    return jnp.transpose(out, (0, 1, 3, 2, 4))


def fits(shape, rows_all, groups):
    rows, kx_local, span_dev = shape
    units = kx_local * (span_dev // LANES)
    return (
        span_dev % LANES == 0
        and units >= groups
        and units % groups == 0
        and rows % EDGE == 0
        and rows_all % LANES == 0
    )


def per_device(velocity, stencil, mode_rates, basis):
    if not fits(velocity.shape[2:], stencil.shape[1], lax.axis_size("gy")):
        return plain_device(velocity, stencil, mode_rates, basis)
    return fast_device(velocity, stencil, mode_rates, basis)


def solution(mesh):
    placed = (P(None, None, "gy", "gx", "gz"), P(), P(), P(("gx", "gz"), None))
    return jax.shard_map(
        per_device,
        mesh=mesh,
        in_specs=placed,
        out_specs=P(None, None, "gy", "gx", "gz"),
        check_vma=False,
    )
```

profile of v0, /device:TPU:0, one launch (start us, length us, event | category | flops | bytes accessed | tf_op | source)
XLA Modules:
  0.0 132.9 jit_solution(14768272609393213011)
XLA Ops:
  0.0 3.9 %collective-permute-start.2 = (f32[96,768]{1,0:T(8,128)}, f32[96,768]{1,0:T(8,128)S(1)}, u32[]{:S(2)}, u32[]{:S(2)}) collective-permute-start(f32[96,768]{1,0:T(8,128)} %refs_0_.1), channel_id=1, source_target_pairs={{0,5},{1,4},{2,7},{3,6},{4,1},{5,0},{6,3},{7,2},{8,13},{9,12},{10,... | collective-permute-start | bytes 884744 | tf_op jit(solution)/shard_map/ppermute | solution.py:233
  5.3 6.8 %collective-permute-done.2.refs_3_ = f32[96,768]{1,0:T(8,128)S(1)} collective-permute-done((f32[96,768]{1,0:T(8,128)}, f32[96,768]{1,0:T(8,128)S(1)}, u32[]{:S(2)}, u32[]{:S(2)}) %collective-permute-start.2) | collective-permute-done | bytes 294944 | tf_op jit(solution)/shard_map/ppermute | solution.py:233
  12.0 5.4 %collective-permute-done.1.refs_2_ = f32[96,768]{1,0:T(8,128)S(1)} collective-permute-done((f32[96,768]{1,0:T(8,128)}, f32[96,768]{1,0:T(8,128)S(1)}, u32[]{:S(2)}, u32[]{:S(2)}) %collective-permute-start.1) | collective-permute-done | bytes 294944 | tf_op jit(solution)/shard_map/ppermute | solution.py:233
  19.4 4.5 %divergence.4 = (f32[392,128]{1,0:T(8,128)}, f32[392,128]{1,0:T(8,128)}, f32[392,128]{1,0:T(8,128)}, f32[392,128]{1,0:T(8,128)}) custom-call(s32[3]{0:T(128)} %pad_add_fusion.place, f32[3,2,6,192,256]{4,3,2,1,0:T(8,128)} %bitcast.5, f32[3,192,128]{2,1,0:T(8,128)} %broadcast_in_dim.4.weights), custom_call_target="tpu_custom_call" | custom-call | flops 2359296 | bytes 4718592 | tf_op jit(solution)/shard_map/divergence/pallas_call | solution.py:290
  25.7 7.5 %collective-permute-done.13.refs_1_ = f32[392,128]{1,0:T(8,128)S(1)} collective-permute-done((f32[392,128]{1,0:T(8,128)}, f32[392,128]{1,0:T(8,128)S(1)}, u32[]{:S(2)}, u32[]{:S(2)}) %collective-permute-start.13) | collective-permute-done | bytes 200736 | tf_op jit(solution)/shard_map/ppermute | solution.py:286
  35.3 4.5 %divergence.5 = (f32[392,128]{1,0:T(8,128)}, f32[392,128]{1,0:T(8,128)}, f32[392,128]{1,0:T(8,128)}, f32[392,128]{1,0:T(8,128)}) custom-call(s32[3]{0:T(128)} %pad_add_fusion.place, f32[3,2,6,192,256]{4,3,2,1,0:T(8,128)} %bitcast.6, f32[3,192,128]{2,1,0:T(8,128)} %broadcast_in_dim.4.weights), custom_call_target="tpu_custom_call" | custom-call | flops 2359296 | bytes 4718592 | tf_op jit(solution)/shard_map/divergence/pallas_call | solution.py:290
  40.4 2.2 %collective-permute-start.20 = (f32[392,128]{1,0:T(8,128)}, f32[392,128]{1,0:T(8,128)}, u32[]{:S(2)}, u32[]{:S(2)}) collective-permute-start(f32[392,128]{1,0:T(8,128)} %get-tuple-element.55), channel_id=1, source_target_pairs={{0,16},{8,24},{16,0},{24,8},{1,17},{9,25},{17,1},{25,9},{2,18},{10... | collective-permute-start | bytes 602120 | tf_op jit(solution)/shard_map/ppermute | solution.py:286
  44.5 4.4 %divergence.3 = (f32[392,128]{1,0:T(8,128)}, f32[392,128]{1,0:T(8,128)}, f32[392,128]{1,0:T(8,128)}, f32[392,128]{1,0:T(8,128)}) custom-call(s32[3]{0:T(128)} %pad_add_fusion.place, f32[3,2,6,192,256]{4,3,2,1,0:T(8,128)} %bitcast.7, f32[3,192,128]{2,1,0:T(8,128)} %broadcast_in_dim.4.weights), custom_call_target="tpu_custom_call" | custom-call | flops 2359296 | bytes 4718592 | tf_op jit(solution)/shard_map/divergence/pallas_call | solution.py:290
  51.3 6.5 %collective-permute-start.8 = (f32[392,128]{1,0:T(8,128)}, f32[392,128]{1,0:T(8,128)S(1)}, u32[]{:S(2)}, u32[]{:S(2)}) collective-permute-start(f32[392,128]{1,0:T(8,128)} %get-tuple-element.39), channel_id=1, source_target_pairs={{0,16},{8,24},{16,0},{24,8},{1,17},{9,25},{17,1},{25,9},{2,18},{10... | collective-permute-start | bytes 602120 | tf_op jit(solution)/shard_map/ppermute | solution.py:286
  57.9 4.7 %solve.4 = (f32[392,128]{1,0:T(8,128)S(1)}, f32[392,128]{1,0:T(8,128)S(1)}, f32[392,128]{1,0:T(8,128)S(1)}, f32[392,128]{1,0:T(8,128)S(1)}) custom-call(s32[3]{0:T(128)S(1)} %copy-done.2, f32[3,768]{1,0:T(4,128)S(1)} %copy-done.3, f32[768,128]{1,0:T(8,128)S(1)} %broadcast_in_dim.5.rates, bf16[768,768]{1,0:T(8,128)(2,1)S(1)} %get-tuple-element.33.high, ...), custom_call_target="tpu_custom_call" | custom-call | flops 1811939328 | bytes 6324224 | tf_op jit(solution)/shard_map/solve/pallas_call | solution.py:327
  62.7 3.6 %collective-permute-start.9 = (f32[392,128]{1,0:T(8,128)S(1)}, f32[392,128]{1,0:T(8,128)S(1)}, u32[]{:S(2)}, u32[]{:S(2)}) collective-permute-start(f32[392,128]{1,0:T(8,128)S(1)} %copy-done.8), channel_id=1, source_target_pairs={{0,24},{8,0},{16,8},{24,16},{1,25},{9,1},{17,9},{25,17},{2,26},{10... | collective-permute-start | bytes 602120 | tf_op jit(solution)/shard_map/ppermute | solution.py:286
  66.2 3.7 %collective-permute-done.20.refs_2_ = f32[392,128]{1,0:T(8,128)} collective-permute-done((f32[392,128]{1,0:T(8,128)}, f32[392,128]{1,0:T(8,128)}, u32[]{:S(2)}, u32[]{:S(2)}) %collective-permute-start.20) | collective-permute-done | bytes 200736 | tf_op jit(solution)/shard_map/ppermute | solution.py:286
  70.0 3.9 %collective-permute-start.16 = (f32[392,128]{1,0:T(8,128)S(1)}, f32[392,128]{1,0:T(8,128)S(1)}, u32[]{:S(2)}, u32[]{:S(2)}) collective-permute-start(f32[392,128]{1,0:T(8,128)S(1)} %get-tuple-element.50), channel_id=1, source_target_pairs={{0,8},{8,16},{16,24},{24,0},{1,9},{9,17},{17,25},{25,1},{2,10},{10... | collective-permute-start | bytes 602120 | tf_op jit(solution)/shard_map/ppermute | solution.py:286
  73.9 5.1 %solve.5 = (f32[392,128]{1,0:T(8,128)S(1)}, f32[392,128]{1,0:T(8,128)S(1)}, f32[392,128]{1,0:T(8,128)S(1)}, f32[392,128]{1,0:T(8,128)S(1)}) custom-call(s32[3]{0:T(128)S(1)} %copy-done.2, f32[3,768]{1,0:T(4,128)S(1)} %copy-done.3, f32[768,128]{1,0:T(8,128)S(1)} %broadcast_in_dim.5.rates, bf16[768,768]{1,0:T(8,128)(2,1)S(1)} %get-tuple-element.33.high, ...), custom_call_target="tpu_custom_call" | custom-call | flops 1811939328 | bytes 6324224 | tf_op jit(solution)/shard_map/solve/pallas_call | solution.py:327
  80.0 2.5 %collective-permute-start.23 = (f32[392,128]{1,0:T(8,128)S(1)}, f32[392,128]{1,0:T(8,128)S(1)}, u32[]{:S(2)}, u32[]{:S(2)}) collective-permute-start(f32[392,128]{1,0:T(8,128)S(1)} %get-tuple-element.59), channel_id=1, source_target_pairs={{0,16},{8,24},{16,0},{24,8},{1,17},{9,25},{17,1},{25,9},{2,18},{10... | collective-permute-start | bytes 602120 | tf_op jit(solution)/shard_map/ppermute | solution.py:286
  82.8 2.6 %collective-permute-start.24 = (f32[392,128]{1,0:T(8,128)S(1)}, f32[392,128]{1,0:T(8,128)S(1)}, u32[]{:S(2)}, u32[]{:S(2)}) collective-permute-start(f32[392,128]{1,0:T(8,128)S(1)} %get-tuple-element.60), channel_id=1, source_target_pairs={{0,24},{8,0},{16,8},{24,16},{1,25},{9,1},{17,9},{25,17},{2,26},{10... | collective-permute-start | bytes 602120 | tf_op jit(solution)/shard_map/ppermute | solution.py:286
  85.4 9.8 %collective-permute-start.17 = (f32[392,128]{1,0:T(8,128)S(1)}, f32[392,128]{1,0:T(8,128)S(1)}, u32[]{:S(2)}, u32[]{:S(2)}) collective-permute-start(f32[392,128]{1,0:T(8,128)S(1)} %get-tuple-element.51), channel_id=1, source_target_pairs={{0,16},{8,24},{16,0},{24,8},{1,17},{9,25},{17,1},{25,9},{2,18},{10... | collective-permute-start | bytes 602120 | tf_op jit(solution)/shard_map/ppermute | solution.py:286
  95.2 4.7 %solve.3 = (f32[392,128]{1,0:T(8,128)S(1)}, f32[392,128]{1,0:T(8,128)S(1)}, f32[392,128]{1,0:T(8,128)S(1)}, f32[392,128]{1,0:T(8,128)S(1)}) custom-call(s32[3]{0:T(128)S(1)} %copy-done.2, f32[3,768]{1,0:T(4,128)S(1)} %copy-done.3, f32[768,128]{1,0:T(8,128)S(1)} %broadcast_in_dim.5.rates, bf16[768,768]{1,0:T(8,128)(2,1)S(1)} %get-tuple-element.33.high, ...), custom_call_target="tpu_custom_call" | custom-call | flops 1811939328 | bytes 6324224 | tf_op jit(solution)/shard_map/solve/pallas_call | solution.py:327
  99.9 3.4 %collective-permute-start.18 = (f32[392,128]{1,0:T(8,128)S(1)}, f32[392,128]{1,0:T(8,128)S(1)}, u32[]{:S(2)}, u32[]{:S(2)}) collective-permute-start(f32[392,128]{1,0:T(8,128)S(1)} %get-tuple-element.52), channel_id=1, source_target_pairs={{0,24},{8,0},{16,8},{24,16},{1,25},{9,1},{17,9},{25,17},{2,26},{10... | collective-permute-start | bytes 602120 | tf_op jit(solution)/shard_map/ppermute | solution.py:286
  105.8 10.2 %collective-permute-start.12 = (f32[392,128]{1,0:T(8,128)S(1)}, f32[392,128]{1,0:T(8,128)S(1)}, u32[]{:S(2)}, u32[]{:S(2)}) collective-permute-start(f32[392,128]{1,0:T(8,128)S(1)} %get-tuple-element.44), channel_id=1, source_target_pairs={{0,24},{8,0},{16,8},{24,16},{1,25},{9,1},{17,9},{25,17},{2,26},{10... | collective-permute-start | bytes 602120 | tf_op jit(solution)/shard_map/ppermute | solution.py:286
  116.1 2.8 %project.3.refs_4_ = f32[3,2,6,192,256]{4,3,2,1,0:T(8,128)} custom-call(s32[3]{0:T(128)S(1)} %copy-done.2, f32[3,2,6,192,256]{4,3,2,1,0:T(8,128)S(1)} %bitcast.10, f32[3,192,128]{2,1,0:T(8,128)S(1)} %copy-done, f32[392,128]{1,0:T(8,128)S(1)} %get-tuple-element.57.refs_0_, f32[392,128]{1,0:T(8,128)S(1)} %collective-permute-done.22.refs_1_, ...), custom_call_target="tpu_custom_call" | custom-call | flops 2359296 | bytes 7077888 | tf_op jit(solution)/shard_map/project/pallas_call | solution.py:370
  121.0 2.8 %project.4.refs_4_ = f32[3,2,6,192,256]{4,3,2,1,0:T(8,128)} custom-call(s32[3]{0:T(128)S(1)} %copy-done.2, f32[3,2,6,192,256]{4,3,2,1,0:T(8,128)S(1)} %bitcast.11, f32[3,192,128]{2,1,0:T(8,128)S(1)} %copy-done, f32[392,128]{1,0:T(8,128)S(1)} %get-tuple-element.49.refs_0_, ...), custom_call_target="tpu_custom_call", output_to_operand_aliasing={{}: (7, {})} | custom-call | flops 2359296 | bytes 7077888 | tf_op jit(solution)/shard_map/project/pallas_call | solution.py:370
  123.8 6.2 %collective-permute-done.11.refs_2_ = f32[392,128]{1,0:T(8,128)S(1)} collective-permute-done((f32[392,128]{1,0:T(8,128)S(1)}, f32[392,128]{1,0:T(8,128)S(1)}, u32[]{:S(2)}, u32[]{:S(2)}) %collective-permute-start.11) | collective-permute-done | bytes 200736 | tf_op jit(solution)/shard_map/ppermute | solution.py:286
  130.1 2.8 %project.5 = f32[3,2,6,192,256]{4,3,2,1,0:T(8,128)} custom-call(s32[3]{0:T(128)S(1)} %copy-done.2, f32[3,2,6,192,256]{4,3,2,1,0:T(8,128)S(1)} %bitcast.12, f32[3,192,128]{2,1,0:T(8,128)S(1)} %copy-done, f32[392,128]{1,0:T(8,128)S(1)} %get-tuple-element.41.refs_0_, f32[392,128]{1,0:T(8,128)S(1)} %collective-permute-done.10.refs_1_, ...), custom_call_target="tpu_custom_call", output_to_operand_aliasing={{}: (7, {})} | custom-call | flops 2359296 | bytes 7077888 | tf_op jit(solution)/shard_map/project/pallas_call | solution.py:370
  (65 shorter events, 18.1 us)
Async XLA Ops:
  0.0 12.0 %collective-permute-start.2 = (f32[96,768]{1,0:T(8,128)}, f32[96,768]{1,0:T(8,128)S(1)}, u32[]{:S(2)}, u32[]{:S(2)}) collective-permute-start(f32[96,768]{1,0:T(8,128)} %refs_0_.1), channel_id=1, source_target_pairs={{0,5},{1,4},{2,7},{3,6},{4,1},{5,0},{6,3},{7,2},{8,13},{9,12},{10,... | collective-permute-start | bytes 884744 | tf_op jit(solution)/shard_map/ppermute | solution.py:233
  3.9 13.5 %collective-permute-start.1 = (f32[96,768]{1,0:T(8,128)}, f32[96,768]{1,0:T(8,128)S(1)}, u32[]{:S(2)}, u32[]{:S(2)}) collective-permute-start(f32[96,768]{1,0:T(8,128)} %refs_0_.1), channel_id=1, source_target_pairs={{0,1},{1,0},{2,3},{3,2},{4,5},{5,4},{6,7},{7,6},{8,9},{9,8},{10,11... | collective-permute-start | bytes 884744 | tf_op jit(solution)/shard_map/ppermute | solution.py:233
  4.4 13.3 %collective-permute-start = (f32[96,768]{1,0:T(8,128)}, f32[96,768]{1,0:T(8,128)S(1)}, u32[]{:S(2)}, u32[]{:S(2)}) collective-permute-start(f32[96,768]{1,0:T(8,128)} %refs_0_.1), channel_id=1, source_target_pairs={{0,4},{1,5},{2,6},{3,7},{4,0},{5,1},{6,2},{7,3},{8,12},{9,13},{10,... | collective-permute-start | bytes 884744 | tf_op jit(solution)/shard_map/ppermute | solution.py:233
  4.5 29.4 %collective-permute-start.3 = (f32[96,768]{1,0:T(8,128)}, f32[96,768]{1,0:T(8,128)S(1)}, u32[]{:S(2)}, u32[]{:S(2)}) collective-permute-start(f32[96,768]{1,0:T(8,128)} %refs_0_.1), channel_id=1, source_target_pairs={{0,2},{1,3},{2,0},{3,1},{4,6},{5,7},{6,4},{7,5},{8,10},{9,11},{10,... | collective-permute-start | bytes 884744 | tf_op jit(solution)/shard_map/ppermute | solution.py:233
  12.0 27.7 %collective-permute-start.6 = (f32[96,768]{1,0:T(8,128)S(1)}, f32[96,768]{1,0:T(8,128)S(1)}, u32[]{:S(2)}, u32[]{:S(2)}) collective-permute-start(f32[96,768]{1,0:T(8,128)S(1)} %collective-permute-done.2.refs_3_), channel_id=1, source_target_pairs={{0,2},{1,3},{2,0},{3,1},{4,6},{5,7},{6,4},{7,5},{8,10},{9,11},{10,... | collective-permute-start | bytes 884744 | tf_op jit(solution)/shard_map/ppermute | solution.py:233
  17.5 22.9 %collective-permute-start.5 = (f32[96,768]{1,0:T(8,128)S(1)}, f32[96,768]{1,0:T(8,128)S(1)}, u32[]{:S(2)}, u32[]{:S(2)}) collective-permute-start(f32[96,768]{1,0:T(8,128)S(1)} %collective-permute-done.1.refs_2_), channel_id=1, source_target_pairs={{0,2},{1,3},{2,0},{3,1},{4,6},{5,7},{6,4},{7,5},{8,10},{9,11},{10,... | collective-permute-start | bytes 884744 | tf_op jit(solution)/shard_map/ppermute | solution.py:233
  17.8 24.8 %collective-permute-start.4 = (f32[96,768]{1,0:T(8,128)S(1)}, f32[96,768]{1,0:T(8,128)S(1)}, u32[]{:S(2)}, u32[]{:S(2)}) collective-permute-start(f32[96,768]{1,0:T(8,128)S(1)} %collective-permute-done.refs_1_), channel_id=1, source_target_pairs={{0,2},{1,3},{2,0},{3,1},{4,6},{5,7},{6,4},{7,5},{8,10},{9,11},{10,... | collective-permute-start | bytes 884744 | tf_op jit(solution)/shard_map/ppermute | solution.py:233
  33.2 18.1 %collective-permute-start.14 = (f32[392,128]{1,0:T(8,128)}, f32[392,128]{1,0:T(8,128)S(1)}, u32[]{:S(2)}, u32[]{:S(2)}) collective-permute-start(f32[392,128]{1,0:T(8,128)} %get-tuple-element.47), channel_id=1, source_target_pairs={{0,16},{8,24},{16,0},{24,8},{1,17},{9,25},{17,1},{25,9},{2,18},{10... | collective-permute-start | bytes 602120 | tf_op jit(solution)/shard_map/ppermute | solution.py:286
  33.9 17.4 %collective-permute-start.15 = (f32[392,128]{1,0:T(8,128)}, f32[392,128]{1,0:T(8,128)S(1)}, u32[]{:S(2)}, u32[]{:S(2)}) collective-permute-start(f32[392,128]{1,0:T(8,128)} %get-tuple-element.48), channel_id=1, source_target_pairs={{0,24},{8,0},{16,8},{24,16},{1,25},{9,1},{17,9},{25,17},{2,26},{10... | collective-permute-start | bytes 602120 | tf_op jit(solution)/shard_map/ppermute | solution.py:286
  39.7 22.9 %collective-permute-start.19 = (f32[392,128]{1,0:T(8,128)}, f32[392,128]{1,0:T(8,128)S(1)}, u32[]{:S(2)}, u32[]{:S(2)}) collective-permute-start(f32[392,128]{1,0:T(8,128)} %get-tuple-element.54), channel_id=1, source_target_pairs={{0,8},{8,16},{16,24},{24,0},{1,9},{9,17},{17,25},{25,1},{2,10},{10... | collective-permute-start | bytes 602120 | tf_op jit(solution)/shard_map/ppermute | solution.py:286
  40.4 29.6 %collective-permute-start.20 = (f32[392,128]{1,0:T(8,128)}, f32[392,128]{1,0:T(8,128)}, u32[]{:S(2)}, u32[]{:S(2)}) collective-permute-start(f32[392,128]{1,0:T(8,128)} %get-tuple-element.55), channel_id=1, source_target_pairs={{0,16},{8,24},{16,0},{24,8},{1,17},{9,25},{17,1},{25,9},{2,18},{10... | collective-permute-start | bytes 602120 | tf_op jit(solution)/shard_map/ppermute | solution.py:286
  42.6 31.3 %collective-permute-start.21 = (f32[392,128]{1,0:T(8,128)}, f32[392,128]{1,0:T(8,128)}, u32[]{:S(2)}, u32[]{:S(2)}) collective-permute-start(f32[392,128]{1,0:T(8,128)} %get-tuple-element.56), channel_id=1, source_target_pairs={{0,24},{8,0},{16,8},{24,16},{1,25},{9,1},{17,9},{25,17},{2,26},{10... | collective-permute-start | bytes 602120 | tf_op jit(solution)/shard_map/ppermute | solution.py:286
  51.3 28.7 %collective-permute-start.7 = (f32[392,128]{1,0:T(8,128)}, f32[392,128]{1,0:T(8,128)S(1)}, u32[]{:S(2)}, u32[]{:S(2)}) collective-permute-start(f32[392,128]{1,0:T(8,128)} %get-tuple-element.38), channel_id=1, source_target_pairs={{0,8},{8,16},{16,24},{24,0},{1,9},{9,17},{17,25},{25,1},{2,10},{10... | collective-permute-start | bytes 602120 | tf_op jit(solution)/shard_map/ppermute | solution.py:286
  51.3 31.5 %collective-permute-start.8 = (f32[392,128]{1,0:T(8,128)}, f32[392,128]{1,0:T(8,128)S(1)}, u32[]{:S(2)}, u32[]{:S(2)}) collective-permute-start(f32[392,128]{1,0:T(8,128)} %get-tuple-element.39), channel_id=1, source_target_pairs={{0,16},{8,24},{16,0},{24,8},{1,17},{9,25},{17,1},{25,9},{2,18},{10... | collective-permute-start | bytes 602120 | tf_op jit(solution)/shard_map/ppermute | solution.py:286
  62.7 22.7 %collective-permute-start.9 = (f32[392,128]{1,0:T(8,128)S(1)}, f32[392,128]{1,0:T(8,128)S(1)}, u32[]{:S(2)}, u32[]{:S(2)}) collective-permute-start(f32[392,128]{1,0:T(8,128)S(1)} %copy-done.8), channel_id=1, source_target_pairs={{0,24},{8,0},{16,8},{24,16},{1,25},{9,1},{17,9},{25,17},{2,26},{10... | collective-permute-start | bytes 602120 | tf_op jit(solution)/shard_map/ppermute | solution.py:286
  70.0 29.9 %collective-permute-start.16 = (f32[392,128]{1,0:T(8,128)S(1)}, f32[392,128]{1,0:T(8,128)S(1)}, u32[]{:S(2)}, u32[]{:S(2)}) collective-permute-start(f32[392,128]{1,0:T(8,128)S(1)} %get-tuple-element.50), channel_id=1, source_target_pairs={{0,8},{8,16},{16,24},{24,0},{1,9},{9,17},{17,25},{25,1},{2,10},{10... | collective-permute-start | bytes 602120 | tf_op jit(solution)/shard_map/ppermute | solution.py:286
  79.0 24.3 %collective-permute-start.22 = (f32[392,128]{1,0:T(8,128)S(1)}, f32[392,128]{1,0:T(8,128)S(1)}, u32[]{:S(2)}, u32[]{:S(2)}) collective-permute-start(f32[392,128]{1,0:T(8,128)S(1)} %get-tuple-element.58), channel_id=1, source_target_pairs={{0,8},{8,16},{16,24},{24,0},{1,9},{9,17},{17,25},{25,1},{2,10},{10... | collective-permute-start | bytes 602120 | tf_op jit(solution)/shard_map/ppermute | solution.py:286
  80.0 24.3 %collective-permute-start.23 = (f32[392,128]{1,0:T(8,128)S(1)}, f32[392,128]{1,0:T(8,128)S(1)}, u32[]{:S(2)}, u32[]{:S(2)}) collective-permute-start(f32[392,128]{1,0:T(8,128)S(1)} %get-tuple-element.59), channel_id=1, source_target_pairs={{0,16},{8,24},{16,0},{24,8},{1,17},{9,25},{17,1},{25,9},{2,18},{10... | collective-permute-start | bytes 602120 | tf_op jit(solution)/shard_map/ppermute | solution.py:286
  82.8 23.1 %collective-permute-start.24 = (f32[392,128]{1,0:T(8,128)S(1)}, f32[392,128]{1,0:T(8,128)S(1)}, u32[]{:S(2)}, u32[]{:S(2)}) collective-permute-start(f32[392,128]{1,0:T(8,128)S(1)} %get-tuple-element.60), channel_id=1, source_target_pairs={{0,24},{8,0},{16,8},{24,16},{1,25},{9,1},{17,9},{25,17},{2,26},{10... | collective-permute-start | bytes 602120 | tf_op jit(solution)/shard_map/ppermute | solution.py:286
  85.4 35.6 %collective-permute-start.17 = (f32[392,128]{1,0:T(8,128)S(1)}, f32[392,128]{1,0:T(8,128)S(1)}, u32[]{:S(2)}, u32[]{:S(2)}) collective-permute-start(f32[392,128]{1,0:T(8,128)S(1)} %get-tuple-element.51), channel_id=1, source_target_pairs={{0,16},{8,24},{16,0},{24,8},{1,17},{9,25},{17,1},{25,9},{2,18},{10... | collective-permute-start | bytes 602120 | tf_op jit(solution)/shard_map/ppermute | solution.py:286
  99.9 21.1 %collective-permute-start.18 = (f32[392,128]{1,0:T(8,128)S(1)}, f32[392,128]{1,0:T(8,128)S(1)}, u32[]{:S(2)}, u32[]{:S(2)}) collective-permute-start(f32[392,128]{1,0:T(8,128)S(1)} %get-tuple-element.52), channel_id=1, source_target_pairs={{0,24},{8,0},{16,8},{24,16},{1,25},{9,1},{17,9},{25,17},{2,26},{10... | collective-permute-start | bytes 602120 | tf_op jit(solution)/shard_map/ppermute | solution.py:286
  103.3 20.5 %collective-permute-start.10 = (f32[392,128]{1,0:T(8,128)S(1)}, f32[392,128]{1,0:T(8,128)S(1)}, u32[]{:S(2)}, u32[]{:S(2)}) collective-permute-start(f32[392,128]{1,0:T(8,128)S(1)} %get-tuple-element.42), channel_id=1, source_target_pairs={{0,8},{8,16},{16,24},{24,0},{1,9},{9,17},{17,25},{25,1},{2,10},{10... | collective-permute-start | bytes 602120 | tf_op jit(solution)/shard_map/ppermute | solution.py:286
  104.3 25.8 %collective-permute-start.11 = (f32[392,128]{1,0:T(8,128)S(1)}, f32[392,128]{1,0:T(8,128)S(1)}, u32[]{:S(2)}, u32[]{:S(2)}) collective-permute-start(f32[392,128]{1,0:T(8,128)S(1)} %get-tuple-element.43), channel_id=1, source_target_pairs={{0,16},{8,24},{16,0},{24,8},{1,17},{9,25},{17,1},{25,9},{2,18},{10... | collective-permute-start | bytes 602120 | tf_op jit(solution)/shard_map/ppermute | solution.py:286
  105.8 24.2 %collective-permute-start.12 = (f32[392,128]{1,0:T(8,128)S(1)}, f32[392,128]{1,0:T(8,128)S(1)}, u32[]{:S(2)}, u32[]{:S(2)}) collective-permute-start(f32[392,128]{1,0:T(8,128)S(1)} %get-tuple-element.44), channel_id=1, source_target_pairs={{0,24},{8,0},{16,8},{24,16},{1,25},{9,1},{17,9},{25,17},{2,26},{10... | collective-permute-start | bytes 602120 | tf_op jit(solution)/shard_map/ppermute | solution.py:286
  (12 other events, 358.2 us)
where the time goes:
time: 135 us; the launch traced here: 133 us
  starting transfers between devices  59 us (44%)
  Pallas kernels  37 us (27%)
  waiting for transfers between devices  34.2 us (25%)
  local copies, waits for them, and re-layouts  1.99 us (1%)
    ppermute x18, starting transfers between devices, exchange(): lax.ppermute(parts[k], 'gy', [(s, (s + k) % groups) for s in range(groups)])  54.2 us
    ppermute x18, waiting for transfers between devices, exchange(): lax.ppermute(parts[k], 'gy', [(s, (s + k) % groups) for s in range(groups)])  21.7 us
    pallas_call x3, Pallas kernels, solve(): pl.pallas_call(functools.partial(solve_kernel, chunk, groups, halves), in...  14.4 us
    pallas_call x3, Pallas kernels, diverge(): pl.pallas_call(functools.partial(divergence_kernel, chunk, groups, halves...  13.4 us
    ppermute x7, waiting for transfers between devices, swap(): lax.ppermute(value, names, [(x * gz + z, (x ^ a) * gz + (z ^ b)) for x in...  12.5 us
    pallas_call x3, Pallas kernels, fast_device(): out = call(place, vel, weights, *returned[chunk], *carried)  8.48 us
    ppermute x7, starting transfers between devices, swap(): lax.ppermute(value, names, [(x * gz + z, (x ^ a) * gz + (z ^ b)) for x in...  4.73 us
  transfers between devices with their start and end apart: 25, of which 10 were waited for; matrix products, arithmetic and copies ran while one was open for 2% of the time, Pallas kernels for 26%

commit v1 on v0

--- a/solution.py
+++ b/solution.py
@@ -106,11 +106,39 @@
     return prev, nxt
 
 
-def divergence_kernel(chunk, groups, halves, place, vel, weights, *outs):
+def pick(shifts, step):
+    value = shifts[0]
+    for at, shift in enumerate(shifts[1:], 1):
+        value = jnp.where(step == at, shift, value)
+    return value
+
+
+def here(groups, chunk, shift):
+    return chunk * groups + lax.rem(lax.axis_index("gy") + shift + groups, groups)
+
+
+def bases(kx_local, span_dev):
+    return None, lax.axis_index("gx") * kx_local, lax.axis_index("gz") * span_dev
+
+
+def divergence_kernel(chunk, groups, halves, sizes, shifts, vel, stencil, *refs):
+    outs, (turned, weights) = refs[: len(shifts)], refs[-2:]
     step = pl.program_id(0)
     rows = vel.shape[3]
-    unit = chunk * groups + lax.rem(place[0] + step, groups)
-    wave_x, wave_z = unit_waves(place, unit, halves, 1)
+    unit = here(groups, chunk, pick(shifts, step))
+    wave_x, wave_z = unit_waves(bases(*sizes), unit, halves, 1)
+
+    @pl.when(step == 0)
+    def _():
+        taps = jnp.concatenate(
+            [stencil[...], jnp.zeros((LANES - 3, stencil.shape[1]), jnp.float32)], 0
+        )
+        turned[...] = taps.T
+        mine = turned[pl.ds(pl.multiple_of(lax.axis_index("gy") * rows, EDGE), rows), :]
+        for tap in range(3):
+            weights[tap] = jnp.broadcast_to(mine[:, tap : tap + 1], (rows, LANES))
+        if len(refs) > len(shifts) + 2:
+            refs[len(shifts)][...] = weights[...]
 
     def write(out):
         edges = []
@@ -125,8 +153,8 @@
         edges.append(jnp.zeros((EDGE - 4, LANES), jnp.float32))
         out[2 * rows :, :] = jnp.concatenate(edges, 0)
 
-    for k in range(groups):
-        pl.when(step == k)(functools.partial(write, outs[k]))
+    for at in range(len(shifts)):
+        pl.when(step == at)(functools.partial(write, outs[at]))
 
 
 def split_kernel(pieces, *refs):
@@ -154,12 +182,12 @@
     return dot(high[...], top) + (dot(high[...], rest) + dot(low[...], top))
 
 
-def solve_kernel(chunk, groups, halves, place, stencil, rates, high, low, high_t, low_t, *refs):
+def solve_kernel(chunk, groups, halves, sizes, stencil, rates, high, low, high_t, low_t, *refs):
     blocks, outs = refs[:groups], refs[groups : 2 * groups]
     field, edge = refs[2 * groups :]
     rows = (blocks[0].shape[0] - EDGE) // 2
     rows_all = high.shape[0]
-    me = place[0]
+    me = lax.axis_index("gy")
     for k in range(groups):
         source = lax.rem(me - k + groups, groups)
         base = pl.multiple_of(source * rows + EDGE, EDGE)
@@ -177,7 +205,7 @@
             field[EDGE + cut - 1 : EDGE + cut, lanes] += stencil[2, cut - 1] * above
             field[EDGE + cut : EDGE + cut + 1, lanes] += stencil[0, cut] * below
     modal = three_products(high, low, field[EDGE : EDGE + rows_all, :])
-    wave_x, wave_z = unit_waves(place, chunk * groups + me, halves, 1)
+    wave_x, wave_z = unit_waves(bases(*sizes), chunk * groups + me, halves, 1)
     scale = -1.0 / (rates[...] + wave_x * wave_x + wave_z * wave_z)
     modal = jnp.concatenate([modal[:, :LANES] * scale, modal[:, LANES:] * scale], 1)
     field[EDGE : EDGE + rows_all, :] = three_products(high_t, low_t, modal)
@@ -196,12 +224,12 @@
         outs[k][2 * rows :, :] = jnp.concatenate(edges, 0)
 
 
-def project_kernel(chunk, groups, halves, place, vel, weights, *refs):
-    blocks, out = refs[:groups], refs[-1]
+def project_kernel(chunk, groups, halves, sizes, shifts, vel, weights, *refs):
+    blocks, out = refs[: len(shifts)], refs[-1]
     step = pl.program_id(0)
     rows = vel.shape[3]
-    unit = chunk * groups + lax.rem(place[0] - step + groups, groups)
-    wave_x, wave_z = unit_waves(place, unit, halves, 1)
+    unit = here(groups, chunk, -pick(shifts, step))
+    wave_x, wave_z = unit_waves(bases(*sizes), unit, halves, 1)
 
     def write(block):
         for part, sign in ((0, 1.0), (1, -1.0)):
@@ -215,8 +243,8 @@
                 weights[0] * prev + weights[1] * press + weights[2] * nxt
             )
 
-    for k in range(groups):
-        pl.when(step == k)(functools.partial(write, blocks[k]))
+    for at in range(len(shifts)):
+        pl.when(step == at)(functools.partial(write, blocks[at]))
 
 
 def shift_order(groups):
@@ -257,25 +285,21 @@
     groups = lax.axis_size("gy")
     halves = span_dev // LANES
     chunks = kx_local * halves // groups
-    me = lax.axis_index("gy")
-    place = jnp.stack(
-        [me, lax.axis_index("gx") * kx_local, lax.axis_index("gz") * span_dev]
-    ).astype(jnp.int32)
+    sizes = (kx_local, span_dev)
     vel = jnp.transpose(velocity, (0, 1, 3, 2, 4))
-    weights = jnp.broadcast_to(
-        lax.dynamic_slice_in_dim(stencil, me * rows, rows, 1)[:, :, None], (3, rows, LANES)
-    )
     block = jax.ShapeDtypeStruct((2 * rows + EDGE, LANES), jnp.float32)
+    taps = jax.ShapeDtypeStruct((3, rows, LANES), jnp.float32)
     whole = pl.BlockSpec(memory_space=pltpu.VMEM)
-    held = pl.BlockSpec(block.shape, lambda i, s: (0, 0))
-    held_weights = pl.BlockSpec(weights.shape, lambda i, s: (0, 0, 0))
+    held = pl.BlockSpec(block.shape, lambda i: (0, 0))
+    held_taps = pl.BlockSpec(taps.shape, lambda i: (0, 0, 0))
     unit_bytes = 6 * rows * LANES * 4
     params = pltpu.CompilerParams(vmem_limit_bytes=40 * 2**20)
     wide_params = pltpu.CompilerParams(vmem_limit_bytes=60 * 2**20)
-
-    def unit_spec(chunk, sign):
-        def index(i, s):
-            unit = chunk * groups + lax.rem(s[0] + sign * i + groups, groups)
+    first = shift_order(groups)
+
+    def unit_spec(chunk, shifts, sign):
+        def index(i):
+            unit = here(groups, chunk, sign * pick(shifts, i))
             return 0, 0, lax.div(unit, halves), 0, lax.rem(unit, halves)
 
         return pl.BlockSpec((3, 2, 1, rows, LANES), index)
@@ -286,26 +310,36 @@
             sent[k] = lax.ppermute(parts[k], "gy", [(s, (s + k) % groups) for s in range(groups)])
         return [sent[k] for k in range(groups)]
 
-    def diverge(chunk):
-        return pl.pallas_call(
-            functools.partial(divergence_kernel, chunk, groups, halves),
-            grid_spec=pltpu.PrefetchScalarGridSpec(
-                num_scalar_prefetch=1,
-                grid=(groups,),
-                in_specs=[unit_spec(chunk, 1), held_weights],
-                out_specs=[held] * groups,
-            ),
-            out_shape=[block] * groups,
+    def diverge(chunk, shifts, with_taps=False):
+        extra = [taps] if with_taps else []
+        outs = pl.pallas_call(
+            functools.partial(divergence_kernel, chunk, groups, halves, sizes, shifts),
+            grid=(len(shifts),),
+            in_specs=[unit_spec(chunk, shifts, 1), pl.BlockSpec(stencil.shape, lambda i: (0, 0))],
+            out_specs=[held] * len(shifts) + [held_taps] * len(extra),
+            out_shape=[block] * len(shifts) + extra,
+            scratch_shapes=[
+                pltpu.VMEM((rows_all, LANES), jnp.float32),
+                pltpu.VMEM(taps.shape, jnp.float32),
+            ],
             compiler_params=wide_params,
             name="divergence",
             cost_estimate=pl.CostEstimate(
-                flops=groups * unit_bytes, bytes_accessed=2 * groups * unit_bytes, transcendentals=0
+                flops=len(shifts) * unit_bytes,
+                bytes_accessed=2 * len(shifts) * unit_bytes,
+                transcendentals=0,
             ),
-        )(place, vel, weights)
+        )(vel, stencil)
+        return dict(zip(shifts, outs)), outs[-1]
 
     arrived = []
     for chunk in range(chunks):
-        parts = diverge(chunk)
+        if chunk == 0:
+            parts, _ = diverge(chunk, first[:1])
+            others, weights = diverge(chunk, first[1:] + [0], True)
+            parts.update(others)
+        else:
+            parts, _ = diverge(chunk, first + [0])
         arrived.append(exchange(parts))
     pieces, rates = gathered_rows(basis, mode_rates)
     rates = jnp.broadcast_to(rates[:, None], (rows_all, LANES))
@@ -325,8 +359,8 @@
 
     def solve(chunk, blocks):
         return pl.pallas_call(
-            functools.partial(solve_kernel, chunk, groups, halves),
-            in_specs=[pl.BlockSpec(memory_space=pltpu.SMEM)] * 2 + [whole] * (5 + groups),
+            functools.partial(solve_kernel, chunk, groups, halves, sizes),
+            in_specs=[pl.BlockSpec(memory_space=pltpu.SMEM)] + [whole] * (5 + groups),
             out_specs=[whole] * groups,
             out_shape=[block] * groups,
             scratch_shapes=[
@@ -340,7 +374,7 @@
                 bytes_accessed=8 * rows_all**2 + 8 * block.size * groups,
                 transcendentals=0,
             ),
-        )(place, stencil, rates, *splits, *blocks)
+        )(stencil, rates, *splits, *blocks)
 
     returned = []
     for chunk in range(chunks):
@@ -348,26 +382,29 @@
         returned.append(exchange(parts))
     out = None
     for chunk in range(chunks):
-        carried = [] if out is None else [out]
-        call = pl.pallas_call(
-            functools.partial(project_kernel, chunk, groups, halves),
-            grid_spec=pltpu.PrefetchScalarGridSpec(
-                num_scalar_prefetch=1,
-                grid=(groups,),
-                in_specs=[unit_spec(chunk, -1), held_weights]
-                + [held] * groups
+        steps = [[0] + first]
+        if chunk == chunks - 1:
+            steps = [[0] + first[:1], first[1:]]
+        for shifts in steps:
+            carried = [] if out is None else [out]
+            call = pl.pallas_call(
+                functools.partial(project_kernel, chunk, groups, halves, sizes, shifts),
+                grid=(len(shifts),),
+                in_specs=[unit_spec(chunk, shifts, -1), held_taps]
+                + [held] * len(shifts)
                 + [pl.BlockSpec(memory_space=pl.ANY)] * len(carried),
-                out_specs=unit_spec(chunk, -1),
-            ),
-            out_shape=jax.ShapeDtypeStruct(vel.shape, jnp.float32),
-            input_output_aliases={3 + groups: 0} if carried else {},
-            compiler_params=params,
-            name="project",
-            cost_estimate=pl.CostEstimate(
-                flops=groups * unit_bytes, bytes_accessed=3 * groups * unit_bytes, transcendentals=0
-            ),
-        )
-        out = call(place, vel, weights, *returned[chunk], *carried)
+                out_specs=unit_spec(chunk, shifts, -1),
+                out_shape=jax.ShapeDtypeStruct(vel.shape, jnp.float32),
+                input_output_aliases={2 + len(shifts): 0} if carried else {},
+                compiler_params=params,
+                name="project",
+                cost_estimate=pl.CostEstimate(
+                    flops=len(shifts) * unit_bytes,
+                    bytes_accessed=3 * len(shifts) * unit_bytes,
+                    transcendentals=0,
+                ),
+            )
+            out = call(vel, weights, *[returned[chunk][k] for k in shifts], *carried)
     return jnp.transpose(out, (0, 1, 3, 2, 4))
 
 

time: 135 us -> 131 us (0.970); the launches traced: 133 us -> 131 us
  waiting for transfers between devices: 34.2 us -> 43.5 us
  starting transfers between devices: 59 us -> 50.6 us
  local copies, waits for them, and re-layouts: 1.99 us -> 0.37 us
    ppermute x18, waiting for transfers between devices: 21.7 us -> 30.2 us  [exchange(): lax.ppermute(parts[k], 'gy', [(s, (s + k) % groups) for s in range(groups)])]
    ppermute x18, starting transfers between devices: 54.2 us -> 45.8 us  [exchange(): lax.ppermute(parts[k], 'gy', [(s, (s + k) % groups) for s in range(groups)])]
    pallas_call x6 -> x7, Pallas kernels: 22.9 us -> 21.7 us  [the longest x3 14.4 us: solve(): pl.pallas_call(functools.partial(solve_kernel, chunk, groups, halves, siz...]
    pallas_call x3 -> x4, Pallas kernels: 13.4 us -> 13.6 us  [diverge(): pl.pallas_call(functools.partial(divergence_kernel, chunk, groups, halves...]
  transfers between devices with their start and end apart: 25 -> 25, of which waited for: 10 -> 7; matrix products, arithmetic and copies ran while one was open for 2% -> 0% of each run, Pallas kernels for 26% -> 27%
where the time goes in v1:
time: 131 us
  starting transfers between devices  50.6 us (39%)
  waiting for transfers between devices  43.5 us (33%)
  Pallas kernels  36.1 us (28%)
    ppermute x18, starting transfers between devices, exchange(): lax.ppermute(parts[k], 'gy', [(s, (s + k) % groups) for s in range(groups)])  45.8 us
    ppermute x18, waiting for transfers between devices, exchange(): lax.ppermute(parts[k], 'gy', [(s, (s + k) % groups) for s in range(groups)])  30.2 us
    pallas_call x3, Pallas kernels, solve(): pl.pallas_call(functools.partial(solve_kernel, chunk, groups, halves, siz...  14.4 us
    pallas_call x4, Pallas kernels, diverge(): pl.pallas_call(functools.partial(divergence_kernel, chunk, groups, halves...  13.6 us
    ppermute x7, waiting for transfers between devices, swap(): lax.ppermute(value, names, [(x * gz + z, (x ^ a) * gz + (z ^ b)) for x in...  13.2 us
    pallas_call x4, Pallas kernels, fast_device(): out = call(vel, weights, *[returned[chunk][k] for k in shifts], *carried)  7.34 us
    ppermute x7, starting transfers between devices, swap(): lax.ppermute(value, names, [(x * gz + z, (x ^ a) * gz + (z ^ b)) for x in...  4.73 us
  transfers between devices with their start and end apart: 25, of which 7 were waited for; matrix products, arithmetic and copies ran while one was open for 0% of the time, Pallas kernels for 27%

profile of v1, /device:TPU:0, one launch (start us, length us, event | category | flops | bytes accessed | tf_op | source)
XLA Modules:
  0.0 130.6 jit_solution(15968550831288182044)
XLA Ops:
  0.0 3.9 %collective-permute-start.2 = (f32[96,768]{1,0:T(8,128)}, f32[96,768]{1,0:T(8,128)S(1)}, u32[]{:S(2)}, u32[]{:S(2)}) collective-permute-start(f32[96,768]{1,0:T(8,128)} %refs_0_.1), channel_id=1, source_target_pairs={{0,5},{1,4},{2,7},{3,6},{4,1},{5,0},{6,3},{7,2},{8,13},{9,12},{10,... | collective-permute-start | bytes 884744 | tf_op jit(solution)/shard_map/ppermute | solution.py:261
  4.5 7.5 %collective-permute-done.2.refs_3_ = f32[96,768]{1,0:T(8,128)S(1)} collective-permute-done((f32[96,768]{1,0:T(8,128)}, f32[96,768]{1,0:T(8,128)S(1)}, u32[]{:S(2)}, u32[]{:S(2)}) %collective-permute-start.2) | collective-permute-done | bytes 294944 | tf_op jit(solution)/shard_map/ppermute | solution.py:261
  12.0 5.4 %collective-permute-done.1.refs_2_ = f32[96,768]{1,0:T(8,128)S(1)} collective-permute-done((f32[96,768]{1,0:T(8,128)}, f32[96,768]{1,0:T(8,128)S(1)}, u32[]{:S(2)}, u32[]{:S(2)}) %collective-permute-start.1) | collective-permute-done | bytes 294944 | tf_op jit(solution)/shard_map/ppermute | solution.py:261
  18.0 3.8 %divergence.6 = (f32[392,128]{1,0:T(8,128)}, f32[392,128]{1,0:T(8,128)}, f32[392,128]{1,0:T(8,128)}, f32[392,128]{1,0:T(8,128)}) custom-call(f32[3,2,6,192,256]{4,3,2,1,0:T(8,128)} %bitcast.2, f32[3,768]{1,0:T(4,128)} %stencil.13), custom_call_target="tpu_custom_call" | custom-call | flops 2359296 | bytes 4718592 | tf_op jit(solution)/shard_map/divergence/pallas_call | solution.py:315
  23.6 7.5 %collective-permute-done.13.refs_1_ = f32[392,128]{1,0:T(8,128)S(1)} collective-permute-done((f32[392,128]{1,0:T(8,128)}, f32[392,128]{1,0:T(8,128)S(1)}, u32[]{:S(2)}, u32[]{:S(2)}) %collective-permute-start.13) | collective-permute-done | bytes 200736 | tf_op jit(solution)/shard_map/ppermute | solution.py:310
  33.1 2.1 %divergence.7 = f32[392,128]{1,0:T(8,128)} custom-call(f32[3,2,6,192,256]{4,3,2,1,0:T(8,128)} %bitcast.3, f32[3,768]{1,0:T(4,128)} %stencil.13), custom_call_target="tpu_custom_call" | custom-call | flops 589824 | bytes 1179648 | tf_op jit(solution)/shard_map/divergence/pallas_call | solution.py:315
  35.3 3.7 %divergence.4 = (f32[392,128]{1,0:T(8,128)}, f32[392,128]{1,0:T(8,128)}, f32[392,128]{1,0:T(8,128)}, f32[3,192,128]{2,1,0:T(8,128)}) custom-call(f32[3,2,6,192,256]{4,3,2,1,0:T(8,128)} %bitcast.4, f32[3,768]{1,0:T(4,128)} %stencil.13), custom_call_target="tpu_custom_call" | custom-call | flops 1769472 | bytes 3538944 | tf_op jit(solution)/shard_map/divergence/pallas_call | solution.py:315
  41.9 2.6 %collective-permute-start.21 = (f32[392,128]{1,0:T(8,128)}, f32[392,128]{1,0:T(8,128)}, u32[]{:S(2)}, u32[]{:S(2)}) collective-permute-start(f32[392,128]{1,0:T(8,128)} %get-tuple-element.56), channel_id=1, source_target_pairs={{0,24},{8,0},{16,8},{24,16},{1,25},{9,1},{17,9},{25,17},{2,26},{10... | collective-permute-start | bytes 602120 | tf_op jit(solution)/shard_map/ppermute | solution.py:310
  44.7 3.9 %divergence.5 = (f32[392,128]{1,0:T(8,128)}, f32[392,128]{1,0:T(8,128)}, f32[392,128]{1,0:T(8,128)}, f32[392,128]{1,0:T(8,128)}) custom-call(f32[3,2,6,192,256]{4,3,2,1,0:T(8,128)} %bitcast.5, f32[3,768]{1,0:T(4,128)} %stencil.13), custom_call_target="tpu_custom_call" | custom-call | flops 2359296 | bytes 4718592 | tf_op jit(solution)/shard_map/divergence/pallas_call | solution.py:315
  49.4 2.6 %collective-permute-start.7 = (f32[392,128]{1,0:T(8,128)}, f32[392,128]{1,0:T(8,128)S(1)}, u32[]{:S(2)}, u32[]{:S(2)}) collective-permute-start(f32[392,128]{1,0:T(8,128)} %get-tuple-element.39), channel_id=1, source_target_pairs={{0,8},{8,16},{16,24},{24,0},{1,9},{9,17},{17,25},{25,1},{2,10},{10... | collective-permute-start | bytes 602120 | tf_op jit(solution)/shard_map/ppermute | solution.py:310
  52.0 4.8 %collective-permute-start.8 = (f32[392,128]{1,0:T(8,128)}, f32[392,128]{1,0:T(8,128)S(1)}, u32[]{:S(2)}, u32[]{:S(2)}) collective-permute-start(f32[392,128]{1,0:T(8,128)} %get-tuple-element.40), channel_id=1, source_target_pairs={{0,16},{8,24},{16,0},{24,8},{1,17},{9,25},{17,1},{25,9},{2,18},{10... | collective-permute-start | bytes 602120 | tf_op jit(solution)/shard_map/ppermute | solution.py:310
  57.0 4.7 %solve.4 = (f32[392,128]{1,0:T(8,128)S(1)}, f32[392,128]{1,0:T(8,128)S(1)}, f32[392,128]{1,0:T(8,128)S(1)}, f32[392,128]{1,0:T(8,128)S(1)}) custom-call(f32[3,768]{1,0:T(4,128)S(1)} %copy-done.2, f32[768,128]{1,0:T(8,128)S(1)} %broadcast_in_dim.2.rates, bf16[768,768]{1,0:T(8,128)(2,1)S(1)} %get-tuple-element.34.high, ...), custom_call_target="tpu_custom_call" | custom-call | flops 1811939328 | bytes 6324224 | tf_op jit(solution)/shard_map/solve/pallas_call | solution.py:361
  61.7 6.0 %collective-permute-done.20.refs_2_ = f32[392,128]{1,0:T(8,128)S(1)} collective-permute-done((f32[392,128]{1,0:T(8,128)}, f32[392,128]{1,0:T(8,128)S(1)}, u32[]{:S(2)}, u32[]{:S(2)}) %collective-permute-start.20) | collective-permute-done | bytes 200736 | tf_op jit(solution)/shard_map/ppermute | solution.py:310
  69.4 5.1 %solve.5 = (f32[392,128]{1,0:T(8,128)S(1)}, f32[392,128]{1,0:T(8,128)S(1)}, f32[392,128]{1,0:T(8,128)S(1)}, f32[392,128]{1,0:T(8,128)S(1)}) custom-call(f32[3,768]{1,0:T(4,128)S(1)} %copy-done.2, f32[768,128]{1,0:T(8,128)S(1)} %broadcast_in_dim.2.rates, bf16[768,768]{1,0:T(8,128)(2,1)S(1)} %get-tuple-element.34.high, ...), custom_call_target="tpu_custom_call" | custom-call | flops 1811939328 | bytes 6324224 | tf_op jit(solution)/shard_map/solve/pallas_call | solution.py:361
  74.5 2.3 %collective-permute-start.22 = (f32[392,128]{1,0:T(8,128)S(1)}, f32[392,128]{1,0:T(8,128)S(1)}, u32[]{:S(2)}, u32[]{:S(2)}) collective-permute-start(f32[392,128]{1,0:T(8,128)S(1)} %get-tuple-element.58), channel_id=1, source_target_pairs={{0,16},{8,24},{16,0},{24,8},{1,17},{9,25},{17,1},{25,9},{2,18},{10... | collective-permute-start | bytes 602120 | tf_op jit(solution)/shard_map/ppermute | solution.py:310
  76.8 7.8 %collective-permute-start.23 = (f32[392,128]{1,0:T(8,128)S(1)}, f32[392,128]{1,0:T(8,128)S(1)}, u32[]{:S(2)}, u32[]{:S(2)}) collective-permute-start(f32[392,128]{1,0:T(8,128)S(1)} %get-tuple-element.59), channel_id=1, source_target_pairs={{0,8},{8,16},{16,24},{24,0},{1,9},{9,17},{17,25},{25,1},{2,10},{10... | collective-permute-start | bytes 602120 | tf_op jit(solution)/shard_map/ppermute | solution.py:310
  84.7 7.1 %collective-permute-start.24 = (f32[392,128]{1,0:T(8,128)S(1)}, f32[392,128]{1,0:T(8,128)S(1)}, u32[]{:S(2)}, u32[]{:S(2)}) collective-permute-start(f32[392,128]{1,0:T(8,128)S(1)} %get-tuple-element.60), channel_id=1, source_target_pairs={{0,24},{8,0},{16,8},{24,16},{1,25},{9,1},{17,9},{25,17},{2,26},{10... | collective-permute-start | bytes 602120 | tf_op jit(solution)/shard_map/ppermute | solution.py:310
  91.8 2.3 %collective-permute-start.17 = (f32[392,128]{1,0:T(8,128)S(1)}, f32[392,128]{1,0:T(8,128)S(1)}, u32[]{:S(2)}, u32[]{:S(2)}) collective-permute-start(f32[392,128]{1,0:T(8,128)S(1)} %get-tuple-element.52), channel_id=1, source_target_pairs={{0,8},{8,16},{16,24},{24,0},{1,9},{9,17},{17,25},{25,1},{2,10},{10... | collective-permute-start | bytes 602120 | tf_op jit(solution)/shard_map/ppermute | solution.py:310
  94.1 8.1 %collective-permute-done.16.refs_1_ = f32[392,128]{1,0:T(8,128)S(1)} collective-permute-done((f32[392,128]{1,0:T(8,128)S(1)}, f32[392,128]{1,0:T(8,128)S(1)}, u32[]{:S(2)}, u32[]{:S(2)}) %collective-permute-start.16) | collective-permute-done | bytes 200736 | tf_op jit(solution)/shard_map/ppermute | solution.py:310
  102.2 4.6 %solve.3 = (f32[392,128]{1,0:T(8,128)S(1)}, f32[392,128]{1,0:T(8,128)S(1)}, f32[392,128]{1,0:T(8,128)S(1)}, f32[392,128]{1,0:T(8,128)S(1)}) custom-call(f32[3,768]{1,0:T(4,128)S(1)} %copy-done.2, f32[768,128]{1,0:T(8,128)S(1)} %broadcast_in_dim.2.rates, bf16[768,768]{1,0:T(8,128)(2,1)S(1)} %get-tuple-element.34.high, ...), custom_call_target="tpu_custom_call" | custom-call | flops 1811939328 | bytes 6324224 | tf_op jit(solution)/shard_map/solve/pallas_call | solution.py:361
  107.0 7.7 %collective-permute-start.10 = (f32[392,128]{1,0:T(8,128)S(1)}, f32[392,128]{1,0:T(8,128)S(1)}, u32[]{:S(2)}, u32[]{:S(2)}) collective-permute-start(f32[392,128]{1,0:T(8,128)S(1)} %get-tuple-element.42), channel_id=1, source_target_pairs={{0,8},{8,16},{16,24},{24,0},{1,9},{9,17},{17,25},{25,1},{2,10},{10... | collective-permute-start | bytes 602120 | tf_op jit(solution)/shard_map/ppermute | solution.py:310
  114.8 2.4 %project.4.refs_4_ = f32[3,2,6,192,256]{4,3,2,1,0:T(8,128)} custom-call(f32[3,2,6,192,256]{4,3,2,1,0:T(8,128)S(1)} %bitcast.8, f32[3,192,128]{2,1,0:T(8,128)S(1)} %copy-done, f32[392,128]{1,0:T(8,128)S(1)} %get-tuple-element.57.refs_0_, f32[392,128]{1,0:T(8,128)S(1)} %collective-permute-done.22.refs_1_, f32[392,128]{1,0:T(8,128)S(1)} %collective-permute-done.23.refs_2_, ...), custom_call_target="tpu_custom_call" | custom-call | flops 2359296 | bytes 7077888 | tf_op jit(solution)/shard_map/project/pallas_call | solution.py:407
  117.1 2.3 %project.5.refs_2_ = f32[3,2,6,192,256]{4,3,2,1,0:T(8,128)} custom-call(f32[3,2,6,192,256]{4,3,2,1,0:T(8,128)S(1)} %bitcast.9, f32[3,192,128]{2,1,0:T(8,128)S(1)} %copy-done, f32[392,128]{1,0:T(8,128)S(1)} %get-tuple-element.50.refs_0_, f32[392,128]{1,0:T(8,128)S(1)} %collective-permute-done.16.refs_1_, ...), custom_call_target="tpu_custom_call", output_to_operand_aliasing={{}: (6, {})} | custom-call | flops 2359296 | bytes 7077888 | tf_op jit(solution)/shard_map/project/pallas_call | solution.py:407
  119.5 8.5 %collective-permute-done.12.refs_1_ = f32[392,128]{1,0:T(8,128)S(1)} collective-permute-done((f32[392,128]{1,0:T(8,128)S(1)}, f32[392,128]{1,0:T(8,128)S(1)}, u32[]{:S(2)}, u32[]{:S(2)}) %collective-permute-start.12) | collective-permute-done | bytes 200736 | tf_op jit(solution)/shard_map/ppermute | solution.py:310
  (62 shorter events, 13.3 us)
Async XLA Ops:
  0.0 12.0 %collective-permute-start.2 = (f32[96,768]{1,0:T(8,128)}, f32[96,768]{1,0:T(8,128)S(1)}, u32[]{:S(2)}, u32[]{:S(2)}) collective-permute-start(f32[96,768]{1,0:T(8,128)} %refs_0_.1), channel_id=1, source_target_pairs={{0,5},{1,4},{2,7},{3,6},{4,1},{5,0},{6,3},{7,2},{8,13},{9,12},{10,... | collective-permute-start | bytes 884744 | tf_op jit(solution)/shard_map/ppermute | solution.py:261
  3.9 13.5 %collective-permute-start.1 = (f32[96,768]{1,0:T(8,128)}, f32[96,768]{1,0:T(8,128)S(1)}, u32[]{:S(2)}, u32[]{:S(2)}) collective-permute-start(f32[96,768]{1,0:T(8,128)} %refs_0_.1), channel_id=1, source_target_pairs={{0,1},{1,0},{2,3},{3,2},{4,5},{5,4},{6,7},{7,6},{8,9},{9,8},{10,11... | collective-permute-start | bytes 884744 | tf_op jit(solution)/shard_map/ppermute | solution.py:261
  4.4 13.3 %collective-permute-start = (f32[96,768]{1,0:T(8,128)}, f32[96,768]{1,0:T(8,128)S(1)}, u32[]{:S(2)}, u32[]{:S(2)}) collective-permute-start(f32[96,768]{1,0:T(8,128)} %refs_0_.1), channel_id=1, source_target_pairs={{0,4},{1,5},{2,6},{3,7},{4,0},{5,1},{6,2},{7,3},{8,12},{9,13},{10,... | collective-permute-start | bytes 884744 | tf_op jit(solution)/shard_map/ppermute | solution.py:261
  4.5 27.3 %collective-permute-start.3 = (f32[96,768]{1,0:T(8,128)}, f32[96,768]{1,0:T(8,128)S(1)}, u32[]{:S(2)}, u32[]{:S(2)}) collective-permute-start(f32[96,768]{1,0:T(8,128)} %refs_0_.1), channel_id=1, source_target_pairs={{0,2},{1,3},{2,0},{3,1},{4,6},{5,7},{6,4},{7,5},{8,10},{9,11},{10,... | collective-permute-start | bytes 884744 | tf_op jit(solution)/shard_map/ppermute | solution.py:261
  12.0 27.0 %collective-permute-start.6 = (f32[96,768]{1,0:T(8,128)S(1)}, f32[96,768]{1,0:T(8,128)S(1)}, u32[]{:S(2)}, u32[]{:S(2)}) collective-permute-start(f32[96,768]{1,0:T(8,128)S(1)} %collective-permute-done.2.refs_3_), channel_id=1, source_target_pairs={{0,2},{1,3},{2,0},{3,1},{4,6},{5,7},{6,4},{7,5},{8,10},{9,11},{10,... | collective-permute-start | bytes 884744 | tf_op jit(solution)/shard_map/ppermute | solution.py:261
  17.5 23.3 %collective-permute-start.5 = (f32[96,768]{1,0:T(8,128)S(1)}, f32[96,768]{1,0:T(8,128)S(1)}, u32[]{:S(2)}, u32[]{:S(2)}) collective-permute-start(f32[96,768]{1,0:T(8,128)S(1)} %collective-permute-done.1.refs_2_), channel_id=1, source_target_pairs={{0,2},{1,3},{2,0},{3,1},{4,6},{5,7},{6,4},{7,5},{8,10},{9,11},{10,... | collective-permute-start | bytes 884744 | tf_op jit(solution)/shard_map/ppermute | solution.py:261
  17.8 24.2 %collective-permute-start.4 = (f32[96,768]{1,0:T(8,128)S(1)}, f32[96,768]{1,0:T(8,128)S(1)}, u32[]{:S(2)}, u32[]{:S(2)}) collective-permute-start(f32[96,768]{1,0:T(8,128)S(1)} %collective-permute-done.refs_1_), channel_id=1, source_target_pairs={{0,2},{1,3},{2,0},{3,1},{4,6},{5,7},{6,4},{7,5},{8,10},{9,11},{10,... | collective-permute-start | bytes 884744 | tf_op jit(solution)/shard_map/ppermute | solution.py:261
  31.1 18.3 %collective-permute-start.14 = (f32[392,128]{1,0:T(8,128)}, f32[392,128]{1,0:T(8,128)S(1)}, u32[]{:S(2)}, u32[]{:S(2)}) collective-permute-start(f32[392,128]{1,0:T(8,128)} %get-tuple-element.48), channel_id=1, source_target_pairs={{0,16},{8,24},{16,0},{24,8},{1,17},{9,25},{17,1},{25,9},{2,18},{10... | collective-permute-start | bytes 602120 | tf_op jit(solution)/shard_map/ppermute | solution.py:310
  31.8 20.2 %collective-permute-start.15 = (f32[392,128]{1,0:T(8,128)}, f32[392,128]{1,0:T(8,128)S(1)}, u32[]{:S(2)}, u32[]{:S(2)}) collective-permute-start(f32[392,128]{1,0:T(8,128)} %get-tuple-element.49), channel_id=1, source_target_pairs={{0,24},{8,0},{16,8},{24,16},{1,25},{9,1},{17,9},{25,17},{2,26},{10... | collective-permute-start | bytes 602120 | tf_op jit(solution)/shard_map/ppermute | solution.py:310
  39.0 28.7 %collective-permute-start.20 = (f32[392,128]{1,0:T(8,128)}, f32[392,128]{1,0:T(8,128)S(1)}, u32[]{:S(2)}, u32[]{:S(2)}) collective-permute-start(f32[392,128]{1,0:T(8,128)} %divergence.7), channel_id=1, source_target_pairs={{0,16},{8,24},{16,0},{24,8},{1,17},{9,25},{17,1},{25,9},{2,18},{10... | collective-permute-start | bytes 602120 | tf_op jit(solution)/shard_map/ppermute | solution.py:310
  40.7 27.0 %collective-permute-start.19 = (f32[392,128]{1,0:T(8,128)}, f32[392,128]{1,0:T(8,128)}, u32[]{:S(2)}, u32[]{:S(2)}) collective-permute-start(f32[392,128]{1,0:T(8,128)} %get-tuple-element.55), channel_id=1, source_target_pairs={{0,8},{8,16},{16,24},{24,0},{1,9},{9,17},{17,25},{25,1},{2,10},{10... | collective-permute-start | bytes 602120 | tf_op jit(solution)/shard_map/ppermute | solution.py:310
  41.9 27.5 %collective-permute-start.21 = (f32[392,128]{1,0:T(8,128)}, f32[392,128]{1,0:T(8,128)}, u32[]{:S(2)}, u32[]{:S(2)}) collective-permute-start(f32[392,128]{1,0:T(8,128)} %get-tuple-element.56), channel_id=1, source_target_pairs={{0,24},{8,0},{16,8},{24,16},{1,25},{9,1},{17,9},{25,17},{2,26},{10... | collective-permute-start | bytes 602120 | tf_op jit(solution)/shard_map/ppermute | solution.py:310
  49.4 27.4 %collective-permute-start.7 = (f32[392,128]{1,0:T(8,128)}, f32[392,128]{1,0:T(8,128)S(1)}, u32[]{:S(2)}, u32[]{:S(2)}) collective-permute-start(f32[392,128]{1,0:T(8,128)} %get-tuple-element.39), channel_id=1, source_target_pairs={{0,8},{8,16},{16,24},{24,0},{1,9},{9,17},{17,25},{25,1},{2,10},{10... | collective-permute-start | bytes 602120 | tf_op jit(solution)/shard_map/ppermute | solution.py:310
  52.0 32.7 %collective-permute-start.8 = (f32[392,128]{1,0:T(8,128)}, f32[392,128]{1,0:T(8,128)S(1)}, u32[]{:S(2)}, u32[]{:S(2)}) collective-permute-start(f32[392,128]{1,0:T(8,128)} %get-tuple-element.40), channel_id=1, source_target_pairs={{0,16},{8,24},{16,0},{24,8},{1,17},{9,25},{17,1},{25,9},{2,18},{10... | collective-permute-start | bytes 602120 | tf_op jit(solution)/shard_map/ppermute | solution.py:310
  67.7 24.1 %collective-permute-start.9 = (f32[392,128]{1,0:T(8,128)S(1)}, f32[392,128]{1,0:T(8,128)S(1)}, u32[]{:S(2)}, u32[]{:S(2)}) collective-permute-start(f32[392,128]{1,0:T(8,128)S(1)} %copy-done.7), channel_id=1, source_target_pairs={{0,24},{8,0},{16,8},{24,16},{1,25},{9,1},{17,9},{25,17},{2,26},{10... | collective-permute-start | bytes 602120 | tf_op jit(solution)/shard_map/ppermute | solution.py:310
  67.7 34.5 %collective-permute-start.16 = (f32[392,128]{1,0:T(8,128)S(1)}, f32[392,128]{1,0:T(8,128)S(1)}, u32[]{:S(2)}, u32[]{:S(2)}) collective-permute-start(f32[392,128]{1,0:T(8,128)S(1)} %get-tuple-element.51), channel_id=1, source_target_pairs={{0,16},{8,24},{16,0},{24,8},{1,17},{9,25},{17,1},{25,9},{2,18},{10... | collective-permute-start | bytes 602120 | tf_op jit(solution)/shard_map/ppermute | solution.py:310
  74.5 32.4 %collective-permute-start.22 = (f32[392,128]{1,0:T(8,128)S(1)}, f32[392,128]{1,0:T(8,128)S(1)}, u32[]{:S(2)}, u32[]{:S(2)}) collective-permute-start(f32[392,128]{1,0:T(8,128)S(1)} %get-tuple-element.58), channel_id=1, source_target_pairs={{0,16},{8,24},{16,0},{24,8},{1,17},{9,25},{17,1},{25,9},{2,18},{10... | collective-permute-start | bytes 602120 | tf_op jit(solution)/shard_map/ppermute | solution.py:310
  76.8 30.1 %collective-permute-start.23 = (f32[392,128]{1,0:T(8,128)S(1)}, f32[392,128]{1,0:T(8,128)S(1)}, u32[]{:S(2)}, u32[]{:S(2)}) collective-permute-start(f32[392,128]{1,0:T(8,128)S(1)} %get-tuple-element.59), channel_id=1, source_target_pairs={{0,8},{8,16},{16,24},{24,0},{1,9},{9,17},{17,25},{25,1},{2,10},{10... | collective-permute-start | bytes 602120 | tf_op jit(solution)/shard_map/ppermute | solution.py:310
  84.7 30.0 %collective-permute-start.24 = (f32[392,128]{1,0:T(8,128)S(1)}, f32[392,128]{1,0:T(8,128)S(1)}, u32[]{:S(2)}, u32[]{:S(2)}) collective-permute-start(f32[392,128]{1,0:T(8,128)S(1)} %get-tuple-element.60), channel_id=1, source_target_pairs={{0,24},{8,0},{16,8},{24,16},{1,25},{9,1},{17,9},{25,17},{2,26},{10... | collective-permute-start | bytes 602120 | tf_op jit(solution)/shard_map/ppermute | solution.py:310
  91.8 25.4 %collective-permute-start.17 = (f32[392,128]{1,0:T(8,128)S(1)}, f32[392,128]{1,0:T(8,128)S(1)}, u32[]{:S(2)}, u32[]{:S(2)}) collective-permute-start(f32[392,128]{1,0:T(8,128)S(1)} %get-tuple-element.52), channel_id=1, source_target_pairs={{0,8},{8,16},{16,24},{24,0},{1,9},{9,17},{17,25},{25,1},{2,10},{10... | collective-permute-start | bytes 602120 | tf_op jit(solution)/shard_map/ppermute | solution.py:310
  102.2 14.9 %collective-permute-start.18 = (f32[392,128]{1,0:T(8,128)S(1)}, f32[392,128]{1,0:T(8,128)S(1)}, u32[]{:S(2)}, u32[]{:S(2)}) collective-permute-start(f32[392,128]{1,0:T(8,128)S(1)} %get-tuple-element.53), channel_id=1, source_target_pairs={{0,24},{8,0},{16,8},{24,16},{1,25},{9,1},{17,9},{25,17},{2,26},{10... | collective-permute-start | bytes 602120 | tf_op jit(solution)/shard_map/ppermute | solution.py:310
  106.9 21.1 %collective-permute-start.12 = (f32[392,128]{1,0:T(8,128)S(1)}, f32[392,128]{1,0:T(8,128)S(1)}, u32[]{:S(2)}, u32[]{:S(2)}) collective-permute-start(f32[392,128]{1,0:T(8,128)S(1)} %get-tuple-element.45), channel_id=1, source_target_pairs={{0,16},{8,24},{16,0},{24,8},{1,17},{9,25},{17,1},{25,9},{2,18},{10... | collective-permute-start | bytes 602120 | tf_op jit(solution)/shard_map/ppermute | solution.py:310
  107.0 22.3 %collective-permute-start.10 = (f32[392,128]{1,0:T(8,128)S(1)}, f32[392,128]{1,0:T(8,128)S(1)}, u32[]{:S(2)}, u32[]{:S(2)}) collective-permute-start(f32[392,128]{1,0:T(8,128)S(1)} %get-tuple-element.42), channel_id=1, source_target_pairs={{0,8},{8,16},{16,24},{24,0},{1,9},{9,17},{17,25},{25,1},{2,10},{10... | collective-permute-start | bytes 602120 | tf_op jit(solution)/shard_map/ppermute | solution.py:310
  114.7 14.6 %collective-permute-start.11 = (f32[392,128]{1,0:T(8,128)S(1)}, f32[392,128]{1,0:T(8,128)S(1)}, u32[]{:S(2)}, u32[]{:S(2)}) collective-permute-start(f32[392,128]{1,0:T(8,128)S(1)} %get-tuple-element.43), channel_id=1, source_target_pairs={{0,24},{8,0},{16,8},{24,16},{1,25},{9,1},{17,9},{25,17},{2,26},{10... | collective-permute-start | bytes 602120 | tf_op jit(solution)/shard_map/ppermute | solution.py:310
  (11 other events, 330.1 us)

commit v2 on v1

--- a/solution.py
+++ b/solution.py
@@ -106,26 +106,26 @@
     return prev, nxt
 
 
-def pick(shifts, step):
-    value = shifts[0]
-    for at, shift in enumerate(shifts[1:], 1):
-        value = jnp.where(step == at, shift, value)
+def pick(flips, step):
+    value = jnp.int32(flips[0])
+    for at, flip in enumerate(flips[1:], 1):
+        value = jnp.where(step == at, jnp.int32(flip), value)
     return value
 
 
-def here(groups, chunk, shift):
-    return chunk * groups + lax.rem(lax.axis_index("gy") + shift + groups, groups)
+def partner(flip):
+    return lax.bitwise_xor(lax.axis_index("gy"), jnp.int32(flip))
 
 
 def bases(kx_local, span_dev):
     return None, lax.axis_index("gx") * kx_local, lax.axis_index("gz") * span_dev
 
 
-def divergence_kernel(chunk, groups, halves, sizes, shifts, vel, stencil, *refs):
-    outs, (turned, weights) = refs[: len(shifts)], refs[-2:]
+def divergence_kernel(chunk, groups, halves, sizes, flips, vel, stencil, *refs):
+    outs, (turned, weights) = refs[: len(flips)], refs[-2:]
     step = pl.program_id(0)
     rows = vel.shape[3]
-    unit = here(groups, chunk, pick(shifts, step))
+    unit = chunk * groups + partner(pick(flips, step))
     wave_x, wave_z = unit_waves(bases(*sizes), unit, halves, 1)
 
     @pl.when(step == 0)
@@ -137,8 +137,8 @@
         mine = turned[pl.ds(pl.multiple_of(lax.axis_index("gy") * rows, EDGE), rows), :]
         for tap in range(3):
             weights[tap] = jnp.broadcast_to(mine[:, tap : tap + 1], (rows, LANES))
-        if len(refs) > len(shifts) + 2:
-            refs[len(shifts)][...] = weights[...]
+        if len(refs) > len(flips) + 2:
+            refs[len(flips)][...] = weights[...]
 
     def write(out):
         edges = []
@@ -153,7 +153,7 @@
         edges.append(jnp.zeros((EDGE - 4, LANES), jnp.float32))
         out[2 * rows :, :] = jnp.concatenate(edges, 0)
 
-    for at in range(len(shifts)):
+    for at in range(len(flips)):
         pl.when(step == at)(functools.partial(write, outs[at]))
 
 
@@ -189,7 +189,7 @@
     rows_all = high.shape[0]
     me = lax.axis_index("gy")
     for k in range(groups):
-        source = lax.rem(me - k + groups, groups)
+        source = partner(k)
         base = pl.multiple_of(source * rows + EDGE, EDGE)
         for part in range(2):
             field[pl.ds(base, rows), part * LANES : (part + 1) * LANES] = blocks[k][
@@ -212,7 +212,7 @@
     field[0:EDGE, :] = jnp.zeros((EDGE, 2 * LANES), jnp.float32)
     field[EDGE + rows_all :, :] = jnp.zeros((EDGE, 2 * LANES), jnp.float32)
     for k in range(groups):
-        target = lax.rem(me + k, groups)
+        target = partner(k)
         start = pl.multiple_of(target * rows, EDGE)
         edges = []
         for part in range(2):
@@ -224,11 +224,11 @@
         outs[k][2 * rows :, :] = jnp.concatenate(edges, 0)
 
 
-def project_kernel(chunk, groups, halves, sizes, shifts, vel, weights, *refs):
-    blocks, out = refs[: len(shifts)], refs[-1]
+def project_kernel(chunk, groups, halves, sizes, flips, vel, weights, *refs):
+    blocks, out = refs[: len(flips)], refs[-1]
     step = pl.program_id(0)
     rows = vel.shape[3]
-    unit = here(groups, chunk, -pick(shifts, step))
+    unit = chunk * groups + partner(pick(flips, step))
     wave_x, wave_z = unit_waves(bases(*sizes), unit, halves, 1)
 
     def write(block):
@@ -243,12 +243,18 @@
                 weights[0] * prev + weights[1] * press + weights[2] * nxt
             )
 
-    for at in range(len(shifts)):
+    for at in range(len(flips)):
         pl.when(step == at)(functools.partial(write, blocks[at]))
 
 
-def shift_order(groups):
-    return sorted(range(1, groups), key=lambda k: abs(2 * k - groups))
+def flip_order(groups):
+    half = groups // 2
+    return [*range(half, groups), *range(1, half)]
+
+
+def last_order(groups):
+    half = groups // 2
+    return [half, *range(1, half), *range(half + 1, groups)]
 
 
 def gathered_rows(basis, mode_rates):
@@ -295,29 +301,32 @@
     unit_bytes = 6 * rows * LANES * 4
     params = pltpu.CompilerParams(vmem_limit_bytes=40 * 2**20)
     wide_params = pltpu.CompilerParams(vmem_limit_bytes=60 * 2**20)
-    first = shift_order(groups)
-
-    def unit_spec(chunk, shifts, sign):
+    first, final = flip_order(groups), last_order(groups)
+
+    def unit_spec(chunk, flips):
         def index(i):
-            unit = here(groups, chunk, sign * pick(shifts, i))
+            unit = chunk * groups + partner(pick(flips, i))
             return 0, 0, lax.div(unit, halves), 0, lax.rem(unit, halves)
 
         return pl.BlockSpec((3, 2, 1, rows, LANES), index)
 
-    def exchange(parts):
+    def exchange(parts, order):
         sent = {0: parts[0]}
-        for k in shift_order(groups):
-            sent[k] = lax.ppermute(parts[k], "gy", [(s, (s + k) % groups) for s in range(groups)])
+        for k in order:
+            sent[k] = lax.ppermute(parts[k], "gy", [(s, s ^ k) for s in range(groups)])
         return [sent[k] for k in range(groups)]
 
-    def diverge(chunk, shifts, with_taps=False):
+    def diverge(chunk, flips, with_taps=False):
         extra = [taps] if with_taps else []
         outs = pl.pallas_call(
-            functools.partial(divergence_kernel, chunk, groups, halves, sizes, shifts),
-            grid=(len(shifts),),
-            in_specs=[unit_spec(chunk, shifts, 1), pl.BlockSpec(stencil.shape, lambda i: (0, 0))],
-            out_specs=[held] * len(shifts) + [held_taps] * len(extra),
-            out_shape=[block] * len(shifts) + extra,
+            functools.partial(divergence_kernel, chunk, groups, halves, sizes, flips),
+            grid=(len(flips),),
+            in_specs=[
+                unit_spec(chunk, flips),
+                pl.BlockSpec(stencil.shape, lambda i: (0, 0)),
+            ],
+            out_specs=[held] * len(flips) + [held_taps] * len(extra),
+            out_shape=[block] * len(flips) + extra,
             scratch_shapes=[
                 pltpu.VMEM((rows_all, LANES), jnp.float32),
                 pltpu.VMEM(taps.shape, jnp.float32),
@@ -325,12 +334,12 @@
             compiler_params=wide_params,
             name="divergence",
             cost_estimate=pl.CostEstimate(
-                flops=len(shifts) * unit_bytes,
-                bytes_accessed=2 * len(shifts) * unit_bytes,
+                flops=len(flips) * unit_bytes,
+                bytes_accessed=2 * len(flips) * unit_bytes,
                 transcendentals=0,
             ),
         )(vel, stencil)
-        return dict(zip(shifts, outs)), outs[-1]
+        return dict(zip(flips, outs)), outs[-1]
 
     arrived = []
     for chunk in range(chunks):
@@ -340,7 +349,7 @@
             parts.update(others)
         else:
             parts, _ = diverge(chunk, first + [0])
-        arrived.append(exchange(parts))
+        arrived.append(exchange(parts, first))
     pieces, rates = gathered_rows(basis, mode_rates)
     rates = jnp.broadcast_to(rates[:, None], (rows_all, LANES))
     matrix = jax.ShapeDtypeStruct((rows_all, rows_all), jnp.bfloat16)
@@ -379,32 +388,32 @@
     returned = []
     for chunk in range(chunks):
         parts = solve(chunk, arrived[chunk])
-        returned.append(exchange(parts))
+        returned.append(exchange(parts, final if chunk == chunks - 1 else first))
     out = None
     for chunk in range(chunks):
         steps = [[0] + first]
         if chunk == chunks - 1:
-            steps = [[0] + first[:1], first[1:]]
-        for shifts in steps:
+            steps = [[0] + final[:1], final[1:-1], final[-1:]]
+        for flips in filter(None, steps):
             carried = [] if out is None else [out]
             call = pl.pallas_call(
-                functools.partial(project_kernel, chunk, groups, halves, sizes, shifts),
-                grid=(len(shifts),),
-                in_specs=[unit_spec(chunk, shifts, -1), held_taps]
-                + [held] * len(shifts)
+                functools.partial(project_kernel, chunk, groups, halves, sizes, flips),
+                grid=(len(flips),),
+                in_specs=[unit_spec(chunk, flips), held_taps]
+                + [held] * len(flips)
                 + [pl.BlockSpec(memory_space=pl.ANY)] * len(carried),
-                out_specs=unit_spec(chunk, shifts, -1),
+                out_specs=unit_spec(chunk, flips),
                 out_shape=jax.ShapeDtypeStruct(vel.shape, jnp.float32),
-                input_output_aliases={2 + len(shifts): 0} if carried else {},
+                input_output_aliases={2 + len(flips): 0} if carried else {},
                 compiler_params=params,
                 name="project",
                 cost_estimate=pl.CostEstimate(
-                    flops=len(shifts) * unit_bytes,
-                    bytes_accessed=3 * len(shifts) * unit_bytes,
+                    flops=len(flips) * unit_bytes,
+                    bytes_accessed=3 * len(flips) * unit_bytes,
                     transcendentals=0,
                 ),
             )
-            out = call(vel, weights, *[returned[chunk][k] for k in shifts], *carried)
+            out = call(vel, weights, *[returned[chunk][k] for k in flips], *carried)
     return jnp.transpose(out, (0, 1, 3, 2, 4))
 
 
@@ -415,6 +424,8 @@
         span_dev % LANES == 0
         and units >= groups
         and units % groups == 0
+        and groups > 1
+        and groups & (groups - 1) == 0
         and rows % EDGE == 0
         and rows_all % LANES == 0
     )

time: 131 us -> 136 us (1.038)
  waiting for transfers between devices: 43.5 us -> 48 us
    ppermute x18, waiting for transfers between devices: 30.2 us -> 34.8 us  [exchange(): sent[k] = lax.ppermute(parts[k], 'gy', [(s, s ^ k) for s in range(groups)])]
    pallas_call x4 -> x5, Pallas kernels: 7.34 us -> 7.84 us  [fast_device(): out = call(vel, weights, *[returned[chunk][k] for k in flips], *carried)]
  transfers between devices with their start and end apart: 25 -> 25, of which waited for: 7 -> 8; matrix products, arithmetic and copies ran while one was open for 0% -> 0% of each run, Pallas kernels for 27% -> 26%
where the time goes in v2:
time: 136 us; the launch traced here: 135 us
  starting transfers between devices  50.3 us (37%)
  waiting for transfers between devices  48 us (35%)
  Pallas kernels  36.6 us (27%)
    ppermute x18, starting transfers between devices, exchange(): sent[k] = lax.ppermute(parts[k], 'gy', [(s, s ^ k) for s in range(groups)])  45.5 us
    ppermute x18, waiting for transfers between devices, exchange(): sent[k] = lax.ppermute(parts[k], 'gy', [(s, s ^ k) for s in range(groups)])  34.8 us
    pallas_call x3, Pallas kernels, solve(): pl.pallas_call(functools.partial(solve_kernel, chunk, groups, halves, siz...  14.4 us
    pallas_call x4, Pallas kernels, diverge(): pl.pallas_call(functools.partial(divergence_kernel, chunk, groups, halves...  13.6 us
    ppermute x7, waiting for transfers between devices, swap(): lax.ppermute(value, names, [(x * gz + z, (x ^ a) * gz + (z ^ b)) for x in...  13.2 us
    pallas_call x5, Pallas kernels, fast_device(): out = call(vel, weights, *[returned[chunk][k] for k in flips], *carried)  7.84 us
    ppermute x7, starting transfers between devices, swap(): lax.ppermute(value, names, [(x * gz + z, (x ^ a) * gz + (z ^ b)) for x in...  4.73 us
  transfers between devices with their start and end apart: 25, of which 8 were waited for; matrix products, arithmetic and copies ran while one was open for 0% of the time, Pallas kernels for 26%

profile of v2, /device:TPU:0, one launch (start us, length us, event | category | flops | bytes accessed | tf_op | source)
XLA Modules:
  0.0 135.4 jit_solution(14029016423449507982)
XLA Ops:
  0.0 3.9 %collective-permute-start.2 = (f32[96,768]{1,0:T(8,128)}, f32[96,768]{1,0:T(8,128)S(1)}, u32[]{:S(2)}, u32[]{:S(2)}) collective-permute-start(f32[96,768]{1,0:T(8,128)} %refs_0_.1), channel_id=1, source_target_pairs={{0,5},{1,4},{2,7},{3,6},{4,1},{5,0},{6,3},{7,2},{8,13},{9,12},{10,... | collective-permute-start | bytes 884744 | tf_op jit(solution)/shard_map/ppermute | solution.py:267
  4.5 7.5 %collective-permute-done.2.refs_3_ = f32[96,768]{1,0:T(8,128)S(1)} collective-permute-done((f32[96,768]{1,0:T(8,128)}, f32[96,768]{1,0:T(8,128)S(1)}, u32[]{:S(2)}, u32[]{:S(2)}) %collective-permute-start.2) | collective-permute-done | bytes 294944 | tf_op jit(solution)/shard_map/ppermute | solution.py:267
  12.0 5.4 %collective-permute-done.1.refs_2_ = f32[96,768]{1,0:T(8,128)S(1)} collective-permute-done((f32[96,768]{1,0:T(8,128)}, f32[96,768]{1,0:T(8,128)S(1)}, u32[]{:S(2)}, u32[]{:S(2)}) %collective-permute-start.1) | collective-permute-done | bytes 294944 | tf_op jit(solution)/shard_map/ppermute | solution.py:267
  18.0 3.8 %divergence.6 = (f32[392,128]{1,0:T(8,128)}, f32[392,128]{1,0:T(8,128)}, f32[392,128]{1,0:T(8,128)}, f32[392,128]{1,0:T(8,128)}) custom-call(f32[3,2,6,192,256]{4,3,2,1,0:T(8,128)} %bitcast.2, f32[3,768]{1,0:T(4,128)} %stencil.13), custom_call_target="tpu_custom_call" | custom-call | flops 2359296 | bytes 4718592 | tf_op jit(solution)/shard_map/divergence/pallas_call | solution.py:321
  23.6 5.6 %collective-permute-done.13.refs_1_ = f32[392,128]{1,0:T(8,128)S(1)} collective-permute-done((f32[392,128]{1,0:T(8,128)}, f32[392,128]{1,0:T(8,128)S(1)}, u32[]{:S(2)}, u32[]{:S(2)}) %collective-permute-start.13) | collective-permute-done | bytes 200736 | tf_op jit(solution)/shard_map/ppermute | solution.py:316
  29.2 2.6 %collective-permute-start.14 = (f32[392,128]{1,0:T(8,128)}, f32[392,128]{1,0:T(8,128)S(1)}, u32[]{:S(2)}, u32[]{:S(2)}) collective-permute-start(f32[392,128]{1,0:T(8,128)} %get-tuple-element.48), channel_id=1, source_target_pairs={{0,16},{8,24},{16,0},{24,8},{1,17},{9,25},{17,1},{25,9},{2,18},{10... | collective-permute-start | bytes 602120 | tf_op jit(solution)/shard_map/ppermute | solution.py:316
  33.1 2.1 %divergence.7 = f32[392,128]{1,0:T(8,128)} custom-call(f32[3,2,6,192,256]{4,3,2,1,0:T(8,128)} %bitcast.3, f32[3,768]{1,0:T(4,128)} %stencil.13), custom_call_target="tpu_custom_call" | custom-call | flops 589824 | bytes 1179648 | tf_op jit(solution)/shard_map/divergence/pallas_call | solution.py:321
  35.3 3.7 %divergence.4 = (f32[392,128]{1,0:T(8,128)}, f32[392,128]{1,0:T(8,128)}, f32[392,128]{1,0:T(8,128)}, f32[3,192,128]{2,1,0:T(8,128)}) custom-call(f32[3,2,6,192,256]{4,3,2,1,0:T(8,128)} %bitcast.4, f32[3,768]{1,0:T(4,128)} %stencil.13), custom_call_target="tpu_custom_call" | custom-call | flops 1769472 | bytes 3538944 | tf_op jit(solution)/shard_map/divergence/pallas_call | solution.py:321
  43.6 4.0 %divergence.5 = (f32[392,128]{1,0:T(8,128)}, f32[392,128]{1,0:T(8,128)}, f32[392,128]{1,0:T(8,128)}, f32[392,128]{1,0:T(8,128)}) custom-call(f32[3,2,6,192,256]{4,3,2,1,0:T(8,128)} %bitcast.5, f32[3,768]{1,0:T(4,128)} %stencil.13), custom_call_target="tpu_custom_call" | custom-call | flops 2359296 | bytes 4718592 | tf_op jit(solution)/shard_map/divergence/pallas_call | solution.py:321
  48.3 3.8 %collective-permute-done.14.refs_2_ = f32[392,128]{1,0:T(8,128)S(1)} collective-permute-done((f32[392,128]{1,0:T(8,128)}, f32[392,128]{1,0:T(8,128)S(1)}, u32[]{:S(2)}, u32[]{:S(2)}) %collective-permute-start.14) | collective-permute-done | bytes 200736 | tf_op jit(solution)/shard_map/ppermute | solution.py:316
  52.1 8.6 %collective-permute-start.8 = (f32[392,128]{1,0:T(8,128)}, f32[392,128]{1,0:T(8,128)S(1)}, u32[]{:S(2)}, u32[]{:S(2)}) collective-permute-start(f32[392,128]{1,0:T(8,128)} %get-tuple-element.40), channel_id=1, source_target_pairs={{0,16},{8,24},{16,0},{24,8},{1,17},{9,25},{17,1},{25,9},{2,18},{10... | collective-permute-start | bytes 602120 | tf_op jit(solution)/shard_map/ppermute | solution.py:316
  60.8 4.7 %solve.4 = (f32[392,128]{1,0:T(8,128)S(1)}, f32[392,128]{1,0:T(8,128)S(1)}, f32[392,128]{1,0:T(8,128)S(1)}, f32[392,128]{1,0:T(8,128)S(1)}) custom-call(f32[3,768]{1,0:T(4,128)S(1)} %copy-done.2, f32[768,128]{1,0:T(8,128)S(1)} %broadcast_in_dim.2.rates, bf16[768,768]{1,0:T(8,128)(2,1)S(1)} %get-tuple-element.34.high, ...), custom_call_target="tpu_custom_call" | custom-call | flops 1811939328 | bytes 6324224 | tf_op jit(solution)/shard_map/solve/pallas_call | solution.py:370
  65.5 2.2 %collective-permute-done.20.refs_2_ = f32[392,128]{1,0:T(8,128)S(1)} collective-permute-done((f32[392,128]{1,0:T(8,128)}, f32[392,128]{1,0:T(8,128)S(1)}, u32[]{:S(2)}, u32[]{:S(2)}) %collective-permute-start.20) | collective-permute-done | bytes 200736 | tf_op jit(solution)/shard_map/ppermute | solution.py:316
  67.7 2.4 %collective-permute-start.9 = (f32[392,128]{1,0:T(8,128)S(1)}, f32[392,128]{1,0:T(8,128)S(1)}, u32[]{:S(2)}, u32[]{:S(2)}) collective-permute-start(f32[392,128]{1,0:T(8,128)S(1)} %copy-done.7), channel_id=1, source_target_pairs={{0,24},{8,16},{16,8},{24,0},{1,25},{9,17},{17,9},{25,1},{2,26},{10... | collective-permute-start | bytes 602120 | tf_op jit(solution)/shard_map/ppermute | solution.py:316
  70.2 5.1 %solve.5 = (f32[392,128]{1,0:T(8,128)S(1)}, f32[392,128]{1,0:T(8,128)S(1)}, f32[392,128]{1,0:T(8,128)S(1)}, f32[392,128]{1,0:T(8,128)S(1)}) custom-call(f32[3,768]{1,0:T(4,128)S(1)} %copy-done.2, f32[768,128]{1,0:T(8,128)S(1)} %broadcast_in_dim.2.rates, bf16[768,768]{1,0:T(8,128)(2,1)S(1)} %get-tuple-element.34.high, ...), custom_call_target="tpu_custom_call" | custom-call | flops 1811939328 | bytes 6324224 | tf_op jit(solution)/shard_map/solve/pallas_call | solution.py:370
  75.3 12.3 %collective-permute-start.22 = (f32[392,128]{1,0:T(8,128)S(1)}, f32[392,128]{1,0:T(8,128)S(1)}, u32[]{:S(2)}, u32[]{:S(2)}) collective-permute-start(f32[392,128]{1,0:T(8,128)S(1)} %get-tuple-element.58), channel_id=1, source_target_pairs={{0,16},{8,24},{16,0},{24,8},{1,17},{9,25},{17,1},{25,9},{2,18},{10... | collective-permute-start | bytes 602120 | tf_op jit(solution)/shard_map/ppermute | solution.py:316
  87.6 3.4 %collective-permute-start.23 = (f32[392,128]{1,0:T(8,128)S(1)}, f32[392,128]{1,0:T(8,128)S(1)}, u32[]{:S(2)}, u32[]{:S(2)}) collective-permute-start(f32[392,128]{1,0:T(8,128)S(1)} %get-tuple-element.59), channel_id=1, source_target_pairs={{0,24},{8,16},{16,8},{24,0},{1,25},{9,17},{17,9},{25,1},{2,26},{10... | collective-permute-start | bytes 602120 | tf_op jit(solution)/shard_map/ppermute | solution.py:316
  91.7 14.8 %collective-permute-done.16.refs_1_ = f32[392,128]{1,0:T(8,128)S(1)} collective-permute-done((f32[392,128]{1,0:T(8,128)S(1)}, f32[392,128]{1,0:T(8,128)S(1)}, u32[]{:S(2)}, u32[]{:S(2)}) %collective-permute-start.16) | collective-permute-done | bytes 200736 | tf_op jit(solution)/shard_map/ppermute | solution.py:316
  106.5 4.7 %solve.3 = (f32[392,128]{1,0:T(8,128)S(1)}, f32[392,128]{1,0:T(8,128)S(1)}, f32[392,128]{1,0:T(8,128)S(1)}, f32[392,128]{1,0:T(8,128)S(1)}) custom-call(f32[3,768]{1,0:T(4,128)S(1)} %copy-done.2, f32[768,128]{1,0:T(8,128)S(1)} %broadcast_in_dim.2.rates, bf16[768,768]{1,0:T(8,128)(2,1)S(1)} %get-tuple-element.34.high, ...), custom_call_target="tpu_custom_call" | custom-call | flops 1811939328 | bytes 6324224 | tf_op jit(solution)/shard_map/solve/pallas_call | solution.py:370
  111.1 3.1 %collective-permute-start.12 = (f32[392,128]{1,0:T(8,128)S(1)}, f32[392,128]{1,0:T(8,128)S(1)}, u32[]{:S(2)}, u32[]{:S(2)}) collective-permute-start(f32[392,128]{1,0:T(8,128)S(1)} %get-tuple-element.45), channel_id=1, source_target_pairs={{0,16},{8,24},{16,0},{24,8},{1,17},{9,25},{17,1},{25,9},{2,18},{10... | collective-permute-start | bytes 602120 | tf_op jit(solution)/shard_map/ppermute | solution.py:316
  114.2 5.1 %collective-permute-start.11 = (f32[392,128]{1,0:T(8,128)S(1)}, f32[392,128]{1,0:T(8,128)S(1)}, u32[]{:S(2)}, u32[]{:S(2)}) collective-permute-start(f32[392,128]{1,0:T(8,128)S(1)} %get-tuple-element.43), channel_id=1, source_target_pairs={{0,8},{8,0},{16,24},{24,16},{1,9},{9,1},{17,25},{25,17},{2,10},{10... | collective-permute-start | bytes 602120 | tf_op jit(solution)/shard_map/ppermute | solution.py:316
  119.3 2.3 %project.5.refs_4_ = f32[3,2,6,192,256]{4,3,2,1,0:T(8,128)} custom-call(f32[3,2,6,192,256]{4,3,2,1,0:T(8,128)S(1)} %bitcast.8, f32[3,192,128]{2,1,0:T(8,128)S(1)} %copy-done, f32[392,128]{1,0:T(8,128)S(1)} %get-tuple-element.57.refs_0_, f32[392,128]{1,0:T(8,128)S(1)} %collective-permute-done.22.refs_1_, f32[392,128]{1,0:T(8,128)S(1)} %collective-permute-done.23.refs_2_, ...), custom_call_target="tpu_custom_call" | custom-call | flops 2359296 | bytes 7077888 | tf_op jit(solution)/shard_map/project/pallas_call | solution.py:416
  121.7 2.3 %project.6.refs_2_ = f32[3,2,6,192,256]{4,3,2,1,0:T(8,128)} custom-call(f32[3,2,6,192,256]{4,3,2,1,0:T(8,128)S(1)} %bitcast.9, f32[3,192,128]{2,1,0:T(8,128)S(1)} %copy-done, f32[392,128]{1,0:T(8,128)S(1)} %get-tuple-element.50.refs_0_, f32[392,128]{1,0:T(8,128)S(1)} %collective-permute-done.16.refs_1_, ...), custom_call_target="tpu_custom_call", output_to_operand_aliasing={{}: (6, {})} | custom-call | flops 2359296 | bytes 7077888 | tf_op jit(solution)/shard_map/project/pallas_call | solution.py:416
  124.0 8.3 %collective-permute-done.12.refs_1_ = f32[392,128]{1,0:T(8,128)S(1)} collective-permute-done((f32[392,128]{1,0:T(8,128)S(1)}, f32[392,128]{1,0:T(8,128)S(1)}, u32[]{:S(2)}, u32[]{:S(2)}) %collective-permute-start.12) | collective-permute-done | bytes 200736 | tf_op jit(solution)/shard_map/ppermute | solution.py:316
  (63 shorter events, 13.5 us)
Async XLA Ops:
  0.0 12.0 %collective-permute-start.2 = (f32[96,768]{1,0:T(8,128)}, f32[96,768]{1,0:T(8,128)S(1)}, u32[]{:S(2)}, u32[]{:S(2)}) collective-permute-start(f32[96,768]{1,0:T(8,128)} %refs_0_.1), channel_id=1, source_target_pairs={{0,5},{1,4},{2,7},{3,6},{4,1},{5,0},{6,3},{7,2},{8,13},{9,12},{10,... | collective-permute-start | bytes 884744 | tf_op jit(solution)/shard_map/ppermute | solution.py:267
  3.9 13.5 %collective-permute-start.1 = (f32[96,768]{1,0:T(8,128)}, f32[96,768]{1,0:T(8,128)S(1)}, u32[]{:S(2)}, u32[]{:S(2)}) collective-permute-start(f32[96,768]{1,0:T(8,128)} %refs_0_.1), channel_id=1, source_target_pairs={{0,1},{1,0},{2,3},{3,2},{4,5},{5,4},{6,7},{7,6},{8,9},{9,8},{10,11... | collective-permute-start | bytes 884744 | tf_op jit(solution)/shard_map/ppermute | solution.py:267
  4.4 13.3 %collective-permute-start = (f32[96,768]{1,0:T(8,128)}, f32[96,768]{1,0:T(8,128)S(1)}, u32[]{:S(2)}, u32[]{:S(2)}) collective-permute-start(f32[96,768]{1,0:T(8,128)} %refs_0_.1), channel_id=1, source_target_pairs={{0,4},{1,5},{2,6},{3,7},{4,0},{5,1},{6,2},{7,3},{8,12},{9,13},{10,... | collective-permute-start | bytes 884744 | tf_op jit(solution)/shard_map/ppermute | solution.py:267
  4.5 27.3 %collective-permute-start.3 = (f32[96,768]{1,0:T(8,128)}, f32[96,768]{1,0:T(8,128)S(1)}, u32[]{:S(2)}, u32[]{:S(2)}) collective-permute-start(f32[96,768]{1,0:T(8,128)} %refs_0_.1), channel_id=1, source_target_pairs={{0,2},{1,3},{2,0},{3,1},{4,6},{5,7},{6,4},{7,5},{8,10},{9,11},{10,... | collective-permute-start | bytes 884744 | tf_op jit(solution)/shard_map/ppermute | solution.py:267
  12.0 27.0 %collective-permute-start.6 = (f32[96,768]{1,0:T(8,128)S(1)}, f32[96,768]{1,0:T(8,128)S(1)}, u32[]{:S(2)}, u32[]{:S(2)}) collective-permute-start(f32[96,768]{1,0:T(8,128)S(1)} %collective-permute-done.2.refs_3_), channel_id=1, source_target_pairs={{0,2},{1,3},{2,0},{3,1},{4,6},{5,7},{6,4},{7,5},{8,10},{9,11},{10,... | collective-permute-start | bytes 884744 | tf_op jit(solution)/shard_map/ppermute | solution.py:267
  17.5 23.2 %collective-permute-start.5 = (f32[96,768]{1,0:T(8,128)S(1)}, f32[96,768]{1,0:T(8,128)S(1)}, u32[]{:S(2)}, u32[]{:S(2)}) collective-permute-start(f32[96,768]{1,0:T(8,128)S(1)} %collective-permute-done.1.refs_2_), channel_id=1, source_target_pairs={{0,2},{1,3},{2,0},{3,1},{4,6},{5,7},{6,4},{7,5},{8,10},{9,11},{10,... | collective-permute-start | bytes 884744 | tf_op jit(solution)/shard_map/ppermute | solution.py:267
  17.8 24.3 %collective-permute-start.4 = (f32[96,768]{1,0:T(8,128)S(1)}, f32[96,768]{1,0:T(8,128)S(1)}, u32[]{:S(2)}, u32[]{:S(2)}) collective-permute-start(f32[96,768]{1,0:T(8,128)S(1)} %collective-permute-done.refs_1_), channel_id=1, source_target_pairs={{0,2},{1,3},{2,0},{3,1},{4,6},{5,7},{6,4},{7,5},{8,10},{9,11},{10,... | collective-permute-start | bytes 884744 | tf_op jit(solution)/shard_map/ppermute | solution.py:267
  29.2 22.9 %collective-permute-start.14 = (f32[392,128]{1,0:T(8,128)}, f32[392,128]{1,0:T(8,128)S(1)}, u32[]{:S(2)}, u32[]{:S(2)}) collective-permute-start(f32[392,128]{1,0:T(8,128)} %get-tuple-element.48), channel_id=1, source_target_pairs={{0,16},{8,24},{16,0},{24,8},{1,17},{9,25},{17,1},{25,9},{2,18},{10... | collective-permute-start | bytes 602120 | tf_op jit(solution)/shard_map/ppermute | solution.py:316
  31.8 20.3 %collective-permute-start.15 = (f32[392,128]{1,0:T(8,128)}, f32[392,128]{1,0:T(8,128)S(1)}, u32[]{:S(2)}, u32[]{:S(2)}) collective-permute-start(f32[392,128]{1,0:T(8,128)} %get-tuple-element.49), channel_id=1, source_target_pairs={{0,24},{8,16},{16,8},{24,0},{1,25},{9,17},{17,9},{25,1},{2,26},{10... | collective-permute-start | bytes 602120 | tf_op jit(solution)/shard_map/ppermute | solution.py:316
  39.0 28.7 %collective-permute-start.20 = (f32[392,128]{1,0:T(8,128)}, f32[392,128]{1,0:T(8,128)S(1)}, u32[]{:S(2)}, u32[]{:S(2)}) collective-permute-start(f32[392,128]{1,0:T(8,128)} %divergence.7), channel_id=1, source_target_pairs={{0,16},{8,24},{16,0},{24,8},{1,17},{9,25},{17,1},{25,9},{2,18},{10... | collective-permute-start | bytes 602120 | tf_op jit(solution)/shard_map/ppermute | solution.py:316
  40.7 29.5 %collective-permute-start.19 = (f32[392,128]{1,0:T(8,128)}, f32[392,128]{1,0:T(8,128)}, u32[]{:S(2)}, u32[]{:S(2)}) collective-permute-start(f32[392,128]{1,0:T(8,128)} %get-tuple-element.55), channel_id=1, source_target_pairs={{0,8},{8,0},{16,24},{24,16},{1,9},{9,1},{17,25},{25,17},{2,10},{10... | collective-permute-start | bytes 602120 | tf_op jit(solution)/shard_map/ppermute | solution.py:316
  42.1 28.1 %collective-permute-start.21 = (f32[392,128]{1,0:T(8,128)}, f32[392,128]{1,0:T(8,128)}, u32[]{:S(2)}, u32[]{:S(2)}) collective-permute-start(f32[392,128]{1,0:T(8,128)} %get-tuple-element.56), channel_id=1, source_target_pairs={{0,24},{8,16},{16,8},{24,0},{1,25},{9,17},{17,9},{25,1},{2,26},{10... | collective-permute-start | bytes 602120 | tf_op jit(solution)/shard_map/ppermute | solution.py:316
  52.1 35.6 %collective-permute-start.7 = (f32[392,128]{1,0:T(8,128)}, f32[392,128]{1,0:T(8,128)S(1)}, u32[]{:S(2)}, u32[]{:S(2)}) collective-permute-start(f32[392,128]{1,0:T(8,128)} %get-tuple-element.39), channel_id=1, source_target_pairs={{0,8},{8,0},{16,24},{24,16},{1,9},{9,1},{17,25},{25,17},{2,10},{10... | collective-permute-start | bytes 602120 | tf_op jit(solution)/shard_map/ppermute | solution.py:316
  52.1 39.0 %collective-permute-start.8 = (f32[392,128]{1,0:T(8,128)}, f32[392,128]{1,0:T(8,128)S(1)}, u32[]{:S(2)}, u32[]{:S(2)}) collective-permute-start(f32[392,128]{1,0:T(8,128)} %get-tuple-element.40), channel_id=1, source_target_pairs={{0,16},{8,24},{16,0},{24,8},{1,17},{9,25},{17,1},{25,9},{2,18},{10... | collective-permute-start | bytes 602120 | tf_op jit(solution)/shard_map/ppermute | solution.py:316
  67.7 23.3 %collective-permute-start.9 = (f32[392,128]{1,0:T(8,128)S(1)}, f32[392,128]{1,0:T(8,128)S(1)}, u32[]{:S(2)}, u32[]{:S(2)}) collective-permute-start(f32[392,128]{1,0:T(8,128)S(1)} %copy-done.7), channel_id=1, source_target_pairs={{0,24},{8,16},{16,8},{24,0},{1,25},{9,17},{17,9},{25,1},{2,26},{10... | collective-permute-start | bytes 602120 | tf_op jit(solution)/shard_map/ppermute | solution.py:316
  70.2 36.3 %collective-permute-start.16 = (f32[392,128]{1,0:T(8,128)S(1)}, f32[392,128]{1,0:T(8,128)S(1)}, u32[]{:S(2)}, u32[]{:S(2)}) collective-permute-start(f32[392,128]{1,0:T(8,128)S(1)} %get-tuple-element.51), channel_id=1, source_target_pairs={{0,16},{8,24},{16,0},{24,8},{1,17},{9,25},{17,1},{25,9},{2,18},{10... | collective-permute-start | bytes 602120 | tf_op jit(solution)/shard_map/ppermute | solution.py:316
  75.3 35.8 %collective-permute-start.22 = (f32[392,128]{1,0:T(8,128)S(1)}, f32[392,128]{1,0:T(8,128)S(1)}, u32[]{:S(2)}, u32[]{:S(2)}) collective-permute-start(f32[392,128]{1,0:T(8,128)S(1)} %get-tuple-element.58), channel_id=1, source_target_pairs={{0,16},{8,24},{16,0},{24,8},{1,17},{9,25},{17,1},{25,9},{2,18},{10... | collective-permute-start | bytes 602120 | tf_op jit(solution)/shard_map/ppermute | solution.py:316
  87.6 26.6 %collective-permute-start.23 = (f32[392,128]{1,0:T(8,128)S(1)}, f32[392,128]{1,0:T(8,128)S(1)}, u32[]{:S(2)}, u32[]{:S(2)}) collective-permute-start(f32[392,128]{1,0:T(8,128)S(1)} %get-tuple-element.59), channel_id=1, source_target_pairs={{0,24},{8,16},{16,8},{24,0},{1,25},{9,17},{17,9},{25,1},{2,26},{10... | collective-permute-start | bytes 602120 | tf_op jit(solution)/shard_map/ppermute | solution.py:316
  91.0 28.2 %collective-permute-start.24 = (f32[392,128]{1,0:T(8,128)S(1)}, f32[392,128]{1,0:T(8,128)S(1)}, u32[]{:S(2)}, u32[]{:S(2)}) collective-permute-start(f32[392,128]{1,0:T(8,128)S(1)} %get-tuple-element.60), channel_id=1, source_target_pairs={{0,8},{8,0},{16,24},{24,16},{1,9},{9,1},{17,25},{25,17},{2,10},{10... | collective-permute-start | bytes 602120 | tf_op jit(solution)/shard_map/ppermute | solution.py:316
  91.0 30.6 %collective-permute-start.17 = (f32[392,128]{1,0:T(8,128)S(1)}, f32[392,128]{1,0:T(8,128)S(1)}, u32[]{:S(2)}, u32[]{:S(2)}) collective-permute-start(f32[392,128]{1,0:T(8,128)S(1)} %get-tuple-element.52), channel_id=1, source_target_pairs={{0,24},{8,16},{16,8},{24,0},{1,25},{9,17},{17,9},{25,1},{2,26},{10... | collective-permute-start | bytes 602120 | tf_op jit(solution)/shard_map/ppermute | solution.py:316
  106.5 15.2 %collective-permute-start.18 = (f32[392,128]{1,0:T(8,128)S(1)}, f32[392,128]{1,0:T(8,128)S(1)}, u32[]{:S(2)}, u32[]{:S(2)}) collective-permute-start(f32[392,128]{1,0:T(8,128)S(1)} %get-tuple-element.53), channel_id=1, source_target_pairs={{0,8},{8,0},{16,24},{24,16},{1,9},{9,1},{17,25},{25,17},{2,10},{10... | collective-permute-start | bytes 602120 | tf_op jit(solution)/shard_map/ppermute | solution.py:316
  111.1 21.1 %collective-permute-start.12 = (f32[392,128]{1,0:T(8,128)S(1)}, f32[392,128]{1,0:T(8,128)S(1)}, u32[]{:S(2)}, u32[]{:S(2)}) collective-permute-start(f32[392,128]{1,0:T(8,128)S(1)} %get-tuple-element.45), channel_id=1, source_target_pairs={{0,16},{8,24},{16,0},{24,8},{1,17},{9,25},{17,1},{25,9},{2,18},{10... | collective-permute-start | bytes 602120 | tf_op jit(solution)/shard_map/ppermute | solution.py:316
  114.2 19.3 %collective-permute-start.11 = (f32[392,128]{1,0:T(8,128)S(1)}, f32[392,128]{1,0:T(8,128)S(1)}, u32[]{:S(2)}, u32[]{:S(2)}) collective-permute-start(f32[392,128]{1,0:T(8,128)S(1)} %get-tuple-element.43), channel_id=1, source_target_pairs={{0,8},{8,0},{16,24},{24,16},{1,9},{9,1},{17,25},{25,17},{2,10},{10... | collective-permute-start | bytes 602120 | tf_op jit(solution)/shard_map/ppermute | solution.py:316
  119.3 15.2 %collective-permute-start.10 = (f32[392,128]{1,0:T(8,128)S(1)}, f32[392,128]{1,0:T(8,128)S(1)}, u32[]{:S(2)}, u32[]{:S(2)}) collective-permute-start(f32[392,128]{1,0:T(8,128)S(1)} %get-tuple-element.42), channel_id=1, source_target_pairs={{0,24},{8,16},{16,8},{24,0},{1,25},{9,17},{17,9},{25,1},{2,26},{10... | collective-permute-start | bytes 602120 | tf_op jit(solution)/shard_map/ppermute | solution.py:316
  (11 other events, 347.3 us)

commit v3 on v2

--- a/solution.py
+++ b/solution.py
@@ -121,37 +121,81 @@
     return None, lax.axis_index("gx") * kx_local, lax.axis_index("gz") * span_dev
 
 
+def make_weights(stencil, turned, weights):
+    rows = weights.shape[1]
+    taps = jnp.concatenate(
+        [stencil[...], jnp.zeros((LANES - 3, stencil.shape[1]), jnp.float32)], 0
+    )
+    turned[...] = taps.T
+    mine = turned[pl.ds(pl.multiple_of(lax.axis_index("gy") * rows, EDGE), rows), :]
+    for tap in range(3):
+        weights[tap] = jnp.broadcast_to(mine[:, tap : tap + 1], (rows, LANES))
+
+
+def write_part(out, part, waves, normal, stream, span, weights):
+    wave_x, wave_z = waves
+    rows = normal.shape[0]
+    prev, nxt = shifted(normal, 0.0, 0.0)
+    out[part * rows : (part + 1) * rows, :] = (-1.0, 1.0)[part] * (
+        wave_x * stream + wave_z * span
+    ) + (weights[0] * prev + weights[1] * normal + weights[2] * nxt)
+    return [normal[0:1, :], normal[rows - 1 :, :]]
+
+
+def write_edges(out, edges):
+    edges.append(jnp.zeros((EDGE - len(edges), LANES), jnp.float32))
+    out[out.shape[0] - EDGE :, :] = jnp.concatenate(edges, 0)
+
+
+def first_kernel(halves, sizes, flip, vel, stencil, out, turned, weights, held, sems):
+    unit = partner(flip)
+    kx, half = lax.div(unit, halves), lax.rem(unit, halves)
+    lanes = pl.ds(pl.multiple_of(half * LANES, LANES), LANES)
+    copies = {}
+    for part in range(2):
+        for kind in range(3):
+            side = part if kind == 1 else 1 - part
+            copies[part, kind] = pltpu.make_async_copy(
+                vel.at[kind, side, kx, :, lanes], held.at[kind, side], sems.at[part, kind]
+            )
+            copies[part, kind].start()
+    make_weights(stencil, turned, weights)
+    waves = unit_waves(bases(*sizes), unit, halves, 1)
+    edges = []
+    for part in range(2):
+        for kind in range(3):
+            copies[part, kind].wait()
+        edges += write_part(
+            out, part, waves, held[1, part], held[0, 1 - part], held[2, 1 - part], weights
+        )
+    write_edges(out, edges)
+
+
 def divergence_kernel(chunk, groups, halves, sizes, flips, vel, stencil, *refs):
     outs, (turned, weights) = refs[: len(flips)], refs[-2:]
     step = pl.program_id(0)
-    rows = vel.shape[3]
     unit = chunk * groups + partner(pick(flips, step))
-    wave_x, wave_z = unit_waves(bases(*sizes), unit, halves, 1)
+    waves = unit_waves(bases(*sizes), unit, halves, 1)
 
     @pl.when(step == 0)
     def _():
-        taps = jnp.concatenate(
-            [stencil[...], jnp.zeros((LANES - 3, stencil.shape[1]), jnp.float32)], 0
-        )
-        turned[...] = taps.T
-        mine = turned[pl.ds(pl.multiple_of(lax.axis_index("gy") * rows, EDGE), rows), :]
-        for tap in range(3):
-            weights[tap] = jnp.broadcast_to(mine[:, tap : tap + 1], (rows, LANES))
+        make_weights(stencil, turned, weights)
         if len(refs) > len(flips) + 2:
             refs[len(flips)][...] = weights[...]
 
     def write(out):
         edges = []
-        for part, sign in ((0, -1.0), (1, 1.0)):
-            normal = vel[1, part, 0]
-            prev, nxt = shifted(normal, 0.0, 0.0)
-            out[part * rows : (part + 1) * rows, :] = (
-                sign * (wave_x * vel[0, 1 - part, 0] + wave_z * vel[2, 1 - part, 0])
-                + (weights[0] * prev + weights[1] * normal + weights[2] * nxt)
+        for part in range(2):
+            edges += write_part(
+                out,
+                part,
+                waves,
+                vel[1, part, 0],
+                vel[0, 1 - part, 0],
+                vel[2, 1 - part, 0],
+                weights,
             )
-            edges += [vel[1, part, 0, 0:1, :], vel[1, part, 0, rows - 1 : rows, :]]
-        edges.append(jnp.zeros((EDGE - 4, LANES), jnp.float32))
-        out[2 * rows :, :] = jnp.concatenate(edges, 0)
+        write_edges(out, edges)
 
     for at in range(len(flips)):
         pl.when(step == at)(functools.partial(write, outs[at]))
@@ -341,10 +385,29 @@
         )(vel, stencil)
         return dict(zip(flips, outs)), outs[-1]
 
+    def begin(flip):
+        return pl.pallas_call(
+            functools.partial(first_kernel, halves, sizes, flip),
+            in_specs=[pl.BlockSpec(memory_space=pl.ANY), whole],
+            out_specs=whole,
+            out_shape=block,
+            scratch_shapes=[
+                pltpu.VMEM((rows_all, LANES), jnp.float32),
+                pltpu.VMEM(taps.shape, jnp.float32),
+                pltpu.VMEM((3, 2, rows, LANES), jnp.float32),
+                pltpu.SemaphoreType.DMA((2, 3)),
+            ],
+            compiler_params=wide_params,
+            name="first",
+            cost_estimate=pl.CostEstimate(
+                flops=unit_bytes, bytes_accessed=2 * unit_bytes, transcendentals=0
+            ),
+        )(vel, stencil)
+
     arrived = []
     for chunk in range(chunks):
         if chunk == 0:
-            parts, _ = diverge(chunk, first[:1])
+            parts = {first[0]: begin(first[0])}
             others, weights = diverge(chunk, first[1:] + [0], True)
             parts.update(others)
         else:
@@ -390,30 +453,28 @@
         parts = solve(chunk, arrived[chunk])
         returned.append(exchange(parts, final if chunk == chunks - 1 else first))
     out = None
-    for chunk in range(chunks):
-        steps = [[0] + first]
-        if chunk == chunks - 1:
-            steps = [[0] + final[:1], final[1:-1], final[-1:]]
-        for flips in filter(None, steps):
-            carried = [] if out is None else [out]
-            call = pl.pallas_call(
-                functools.partial(project_kernel, chunk, groups, halves, sizes, flips),
-                grid=(len(flips),),
-                in_specs=[unit_spec(chunk, flips), held_taps]
-                + [held] * len(flips)
-                + [pl.BlockSpec(memory_space=pl.ANY)] * len(carried),
-                out_specs=unit_spec(chunk, flips),
-                out_shape=jax.ShapeDtypeStruct(vel.shape, jnp.float32),
-                input_output_aliases={2 + len(flips): 0} if carried else {},
-                compiler_params=params,
-                name="project",
-                cost_estimate=pl.CostEstimate(
-                    flops=len(flips) * unit_bytes,
-                    bytes_accessed=3 * len(flips) * unit_bytes,
-                    transcendentals=0,
-                ),
-            )
-            out = call(vel, weights, *[returned[chunk][k] for k in flips], *carried)
+    steps = [(chunk, [0] + first) for chunk in range(chunks - 1)]
+    steps = [(chunks - 1, [0])] + steps + [(chunks - 1, [k]) for k in final]
+    for chunk, flips in steps:
+        carried = [] if out is None else [out]
+        call = pl.pallas_call(
+            functools.partial(project_kernel, chunk, groups, halves, sizes, flips),
+            grid=(len(flips),),
+            in_specs=[unit_spec(chunk, flips), held_taps]
+            + [held] * len(flips)
+            + [pl.BlockSpec(memory_space=pl.ANY)] * len(carried),
+            out_specs=unit_spec(chunk, flips),
+            out_shape=jax.ShapeDtypeStruct(vel.shape, jnp.float32),
+            input_output_aliases={2 + len(flips): 0} if carried else {},
+            compiler_params=params,
+            name="project",
+            cost_estimate=pl.CostEstimate(
+                flops=len(flips) * unit_bytes,
+                bytes_accessed=3 * len(flips) * unit_bytes,
+                transcendentals=0,
+            ),
+        )
+        out = call(vel, weights, *[returned[chunk][k] for k in flips], *carried)
     return jnp.transpose(out, (0, 1, 3, 2, 4))
 
 

time: 136 us -> 135 us (level)
    pallas_call x0 -> x1, Pallas kernels: none -> 2.63 us  [begin(): pl.pallas_call(functools.partial(first_kernel, halves, sizes, flip), in_s...]
    pallas_call x4 -> x3, Pallas kernels: 13.6 us -> 11.6 us  [diverge(): pl.pallas_call(functools.partial(divergence_kernel, chunk, groups, halves...]
    pallas_call x5 -> x6, Pallas kernels: 7.84 us -> 8.4 us  [fast_device(): out = call(vel, weights, *[returned[chunk][k] for k in flips], *carried)]
  transfers between devices with their start and end apart: 25 -> 25, of which waited for: 8 -> 8; matrix products, arithmetic and copies ran while one was open for 0% -> 0% of each run, Pallas kernels for 26% -> 27%
where the time goes in v3:
time: 135 us
  starting transfers between devices  50 us (37%)
  waiting for transfers between devices  46.7 us (35%)
  Pallas kernels  37.8 us (28%)
    ppermute x18, starting transfers between devices, exchange(): sent[k] = lax.ppermute(parts[k], 'gy', [(s, s ^ k) for s in range(groups)])  45.2 us
    ppermute x18, waiting for transfers between devices, exchange(): sent[k] = lax.ppermute(parts[k], 'gy', [(s, s ^ k) for s in range(groups)])  33.5 us
    pallas_call x3, Pallas kernels, solve(): pl.pallas_call(functools.partial(solve_kernel, chunk, groups, halves, siz...  14.4 us
    ppermute x7, waiting for transfers between devices, swap(): lax.ppermute(value, names, [(x * gz + z, (x ^ a) * gz + (z ^ b)) for x in...  13.2 us
    pallas_call x3, Pallas kernels, diverge(): pl.pallas_call(functools.partial(divergence_kernel, chunk, groups, halves...  11.6 us
    pallas_call x6, Pallas kernels, fast_device(): out = call(vel, weights, *[returned[chunk][k] for k in flips], *carried)  8.4 us
    ppermute x7, starting transfers between devices, swap(): lax.ppermute(value, names, [(x * gz + z, (x ^ a) * gz + (z ^ b)) for x in...  4.73 us
  transfers between devices with their start and end apart: 25, of which 8 were waited for; matrix products, arithmetic and copies ran while one was open for 0% of the time, Pallas kernels for 27%

profile of v3, /device:TPU:0, one launch (start us, length us, event | category | flops | bytes accessed | tf_op | source)
XLA Modules:
  0.0 135.1 jit_solution(13017548309701270288)
XLA Ops:
  0.0 3.9 %collective-permute-start.2 = (f32[96,768]{1,0:T(8,128)}, f32[96,768]{1,0:T(8,128)S(1)}, u32[]{:S(2)}, u32[]{:S(2)}) collective-permute-start(f32[96,768]{1,0:T(8,128)} %refs_0_.1), channel_id=1, source_target_pairs={{0,5},{1,4},{2,7},{3,6},{4,1},{5,0},{6,3},{7,2},{8,13},{9,12},{10,... | collective-permute-start | bytes 884744 | tf_op jit(solution)/shard_map/ppermute | solution.py:311
  4.5 7.5 %collective-permute-done.2.refs_3_ = f32[96,768]{1,0:T(8,128)S(1)} collective-permute-done((f32[96,768]{1,0:T(8,128)}, f32[96,768]{1,0:T(8,128)S(1)}, u32[]{:S(2)}, u32[]{:S(2)}) %collective-permute-start.2) | collective-permute-done | bytes 294944 | tf_op jit(solution)/shard_map/ppermute | solution.py:311
  12.0 5.4 %collective-permute-done.1.refs_2_ = f32[96,768]{1,0:T(8,128)S(1)} collective-permute-done((f32[96,768]{1,0:T(8,128)}, f32[96,768]{1,0:T(8,128)S(1)}, u32[]{:S(2)}, u32[]{:S(2)}) %collective-permute-start.1) | collective-permute-done | bytes 294944 | tf_op jit(solution)/shard_map/ppermute | solution.py:311
  18.0 3.8 %divergence.5 = (f32[392,128]{1,0:T(8,128)}, f32[392,128]{1,0:T(8,128)}, f32[392,128]{1,0:T(8,128)}, f32[392,128]{1,0:T(8,128)}) custom-call(f32[3,2,6,192,256]{4,3,2,1,0:T(8,128)} %bitcast.2, f32[3,768]{1,0:T(4,128)} %stencil.13), custom_call_target="tpu_custom_call" | custom-call | flops 2359296 | bytes 4718592 | tf_op jit(solution)/shard_map/divergence/pallas_call | solution.py:365
  23.6 5.6 %collective-permute-done.13.refs_1_ = f32[392,128]{1,0:T(8,128)S(1)} collective-permute-done((f32[392,128]{1,0:T(8,128)}, f32[392,128]{1,0:T(8,128)S(1)}, u32[]{:S(2)}, u32[]{:S(2)}) %collective-permute-start.13) | collective-permute-done | bytes 200736 | tf_op jit(solution)/shard_map/ppermute | solution.py:360
  29.2 2.6 %collective-permute-start.14 = (f32[392,128]{1,0:T(8,128)}, f32[392,128]{1,0:T(8,128)S(1)}, u32[]{:S(2)}, u32[]{:S(2)}) collective-permute-start(f32[392,128]{1,0:T(8,128)} %get-tuple-element.47), channel_id=1, source_target_pairs={{0,16},{8,24},{16,0},{24,8},{1,17},{9,25},{17,1},{25,9},{2,18},{10... | collective-permute-start | bytes 602120 | tf_op jit(solution)/shard_map/ppermute | solution.py:360
  33.1 2.6 %first.1 = f32[392,128]{1,0:T(8,128)} custom-call(f32[3,2,6,192,256]{4,3,2,1,0:T(8,128)} %bitcast.3, f32[3,768]{1,0:T(4,128)} %stencil.13), custom_call_target="tpu_custom_call" | custom-call | flops 589824 | bytes 1179648 | tf_op jit(solution)/shard_map/first/pallas_call | solution.py:389
  35.8 3.8 %divergence.3 = (f32[392,128]{1,0:T(8,128)}, f32[392,128]{1,0:T(8,128)}, f32[392,128]{1,0:T(8,128)}, f32[3,192,128]{2,1,0:T(8,128)}) custom-call(f32[3,2,6,192,256]{4,3,2,1,0:T(8,128)} %bitcast.4, f32[3,768]{1,0:T(4,128)} %stencil.13), custom_call_target="tpu_custom_call" | custom-call | flops 1769472 | bytes 3538944 | tf_op jit(solution)/shard_map/divergence/pallas_call | solution.py:365
  44.2 4.0 %divergence.4 = (f32[392,128]{1,0:T(8,128)}, f32[392,128]{1,0:T(8,128)}, f32[392,128]{1,0:T(8,128)}, f32[392,128]{1,0:T(8,128)}) custom-call(f32[3,2,6,192,256]{4,3,2,1,0:T(8,128)} %bitcast.5, f32[3,768]{1,0:T(4,128)} %stencil.13), custom_call_target="tpu_custom_call" | custom-call | flops 2359296 | bytes 4718592 | tf_op jit(solution)/shard_map/divergence/pallas_call | solution.py:365
  48.9 3.4 %collective-permute-done.14.refs_2_ = f32[392,128]{1,0:T(8,128)S(1)} collective-permute-done((f32[392,128]{1,0:T(8,128)}, f32[392,128]{1,0:T(8,128)S(1)}, u32[]{:S(2)}, u32[]{:S(2)}) %collective-permute-start.14) | collective-permute-done | bytes 200736 | tf_op jit(solution)/shard_map/ppermute | solution.py:360
  52.4 8.3 %collective-permute-start.8 = (f32[392,128]{1,0:T(8,128)}, f32[392,128]{1,0:T(8,128)S(1)}, u32[]{:S(2)}, u32[]{:S(2)}) collective-permute-start(f32[392,128]{1,0:T(8,128)} %get-tuple-element.40), channel_id=1, source_target_pairs={{0,16},{8,24},{16,0},{24,8},{1,17},{9,25},{17,1},{25,9},{2,18},{10... | collective-permute-start | bytes 602120 | tf_op jit(solution)/shard_map/ppermute | solution.py:360
  60.8 4.7 %solve.4 = (f32[392,128]{1,0:T(8,128)S(1)}, f32[392,128]{1,0:T(8,128)S(1)}, f32[392,128]{1,0:T(8,128)S(1)}, f32[392,128]{1,0:T(8,128)S(1)}) custom-call(f32[3,768]{1,0:T(4,128)S(1)} %copy-done.2, f32[768,128]{1,0:T(8,128)S(1)} %broadcast_in_dim.2.rates, bf16[768,768]{1,0:T(8,128)(2,1)S(1)} %get-tuple-element.34.high, ...), custom_call_target="tpu_custom_call" | custom-call | flops 1811939328 | bytes 6324224 | tf_op jit(solution)/shard_map/solve/pallas_call | solution.py:433
  65.5 2.2 %collective-permute-done.20.refs_2_ = f32[392,128]{1,0:T(8,128)S(1)} collective-permute-done((f32[392,128]{1,0:T(8,128)}, f32[392,128]{1,0:T(8,128)S(1)}, u32[]{:S(2)}, u32[]{:S(2)}) %collective-permute-start.20) | collective-permute-done | bytes 200736 | tf_op jit(solution)/shard_map/ppermute | solution.py:360
  67.7 2.5 %collective-permute-start.9 = (f32[392,128]{1,0:T(8,128)S(1)}, f32[392,128]{1,0:T(8,128)S(1)}, u32[]{:S(2)}, u32[]{:S(2)}) collective-permute-start(f32[392,128]{1,0:T(8,128)S(1)} %copy-done.7), channel_id=1, source_target_pairs={{0,24},{8,16},{16,8},{24,0},{1,25},{9,17},{17,9},{25,1},{2,26},{10... | collective-permute-start | bytes 602120 | tf_op jit(solution)/shard_map/ppermute | solution.py:360
  70.2 5.1 %solve.5 = (f32[392,128]{1,0:T(8,128)S(1)}, f32[392,128]{1,0:T(8,128)S(1)}, f32[392,128]{1,0:T(8,128)S(1)}, f32[392,128]{1,0:T(8,128)S(1)}) custom-call(f32[3,768]{1,0:T(4,128)S(1)} %copy-done.2, f32[768,128]{1,0:T(8,128)S(1)} %broadcast_in_dim.2.rates, bf16[768,768]{1,0:T(8,128)(2,1)S(1)} %get-tuple-element.34.high, ...), custom_call_target="tpu_custom_call" | custom-call | flops 1811939328 | bytes 6324224 | tf_op jit(solution)/shard_map/solve/pallas_call | solution.py:433
  75.3 12.3 %collective-permute-start.22 = (f32[392,128]{1,0:T(8,128)S(1)}, f32[392,128]{1,0:T(8,128)S(1)}, u32[]{:S(2)}, u32[]{:S(2)}) collective-permute-start(f32[392,128]{1,0:T(8,128)S(1)} %get-tuple-element.57), channel_id=1, source_target_pairs={{0,16},{8,24},{16,0},{24,8},{1,17},{9,25},{17,1},{25,9},{2,18},{10... | collective-permute-start | bytes 602120 | tf_op jit(solution)/shard_map/ppermute | solution.py:360
  87.6 3.4 %collective-permute-start.23 = (f32[392,128]{1,0:T(8,128)S(1)}, f32[392,128]{1,0:T(8,128)S(1)}, u32[]{:S(2)}, u32[]{:S(2)}) collective-permute-start(f32[392,128]{1,0:T(8,128)S(1)} %get-tuple-element.58), channel_id=1, source_target_pairs={{0,24},{8,16},{16,8},{24,0},{1,25},{9,17},{17,9},{25,1},{2,26},{10... | collective-permute-start | bytes 602120 | tf_op jit(solution)/shard_map/ppermute | solution.py:360
  91.7 14.8 %collective-permute-done.16.refs_1_ = f32[392,128]{1,0:T(8,128)S(1)} collective-permute-done((f32[392,128]{1,0:T(8,128)S(1)}, f32[392,128]{1,0:T(8,128)S(1)}, u32[]{:S(2)}, u32[]{:S(2)}) %collective-permute-start.16) | collective-permute-done | bytes 200736 | tf_op jit(solution)/shard_map/ppermute | solution.py:360
  106.5 4.7 %solve.3 = (f32[392,128]{1,0:T(8,128)S(1)}, f32[392,128]{1,0:T(8,128)S(1)}, f32[392,128]{1,0:T(8,128)S(1)}, f32[392,128]{1,0:T(8,128)S(1)}) custom-call(f32[3,768]{1,0:T(4,128)S(1)} %copy-done.2, f32[768,128]{1,0:T(8,128)S(1)} %broadcast_in_dim.2.rates, bf16[768,768]{1,0:T(8,128)(2,1)S(1)} %get-tuple-element.34.high, ...), custom_call_target="tpu_custom_call" | custom-call | flops 1811939328 | bytes 6324224 | tf_op jit(solution)/shard_map/solve/pallas_call | solution.py:433
  111.1 3.1 %collective-permute-start.12 = (f32[392,128]{1,0:T(8,128)S(1)}, f32[392,128]{1,0:T(8,128)S(1)}, u32[]{:S(2)}, u32[]{:S(2)}) collective-permute-start(f32[392,128]{1,0:T(8,128)S(1)} %get-tuple-element.44), channel_id=1, source_target_pairs={{0,16},{8,24},{16,0},{24,8},{1,17},{9,25},{17,1},{25,9},{2,18},{10... | collective-permute-start | bytes 602120 | tf_op jit(solution)/shard_map/ppermute | solution.py:360
  114.2 5.0 %collective-permute-start.11 = (f32[392,128]{1,0:T(8,128)S(1)}, f32[392,128]{1,0:T(8,128)S(1)}, u32[]{:S(2)}, u32[]{:S(2)}) collective-permute-start(f32[392,128]{1,0:T(8,128)S(1)} %get-tuple-element.43), channel_id=1, source_target_pairs={{0,8},{8,0},{16,24},{24,16},{1,9},{9,1},{17,25},{25,17},{2,10},{10... | collective-permute-start | bytes 602120 | tf_op jit(solution)/shard_map/ppermute | solution.py:360
  120.2 2.3 %project.7.refs_4_ = f32[3,2,6,192,256]{4,3,2,1,0:T(8,128)} custom-call(f32[3,2,6,192,256]{4,3,2,1,0:T(8,128)S(1)} %bitcast.9, f32[3,192,128]{2,1,0:T(8,128)S(1)} %copy-done, f32[392,128]{1,0:T(8,128)S(1)} %get-tuple-element.56.refs_0_, f32[392,128]{1,0:T(8,128)S(1)} %collective-permute-done.22.refs_1_, ...), custom_call_target="tpu_custom_call", output_to_operand_aliasing={{}: (6, {})} | custom-call | flops 2359296 | bytes 7077888 | tf_op jit(solution)/shard_map/project/pallas_call | solution.py:477
  122.4 2.4 %project.8.refs_1_ = f32[3,2,6,192,256]{4,3,2,1,0:T(8,128)} custom-call(f32[3,2,6,192,256]{4,3,2,1,0:T(8,128)S(1)} %bitcast.10, f32[3,192,128]{2,1,0:T(8,128)S(1)} %copy-done, f32[392,128]{1,0:T(8,128)S(1)} %get-tuple-element.49.refs_0_, f32[392,128]{1,0:T(8,128)S(1)} %collective-permute-done.16.refs_1_, ...), custom_call_target="tpu_custom_call", output_to_operand_aliasing={{}: (6, {})} | custom-call | flops 2359296 | bytes 7077888 | tf_op jit(solution)/shard_map/project/pallas_call | solution.py:477
  124.8 7.4 %collective-permute-done.12.refs_0_ = f32[392,128]{1,0:T(8,128)S(1)} collective-permute-done((f32[392,128]{1,0:T(8,128)S(1)}, f32[392,128]{1,0:T(8,128)S(1)}, u32[]{:S(2)}, u32[]{:S(2)}) %collective-permute-start.12) | collective-permute-done | bytes 200736 | tf_op jit(solution)/shard_map/ppermute | solution.py:360
  (64 shorter events, 14.3 us)
Async XLA Ops:
  0.0 12.0 %collective-permute-start.2 = (f32[96,768]{1,0:T(8,128)}, f32[96,768]{1,0:T(8,128)S(1)}, u32[]{:S(2)}, u32[]{:S(2)}) collective-permute-start(f32[96,768]{1,0:T(8,128)} %refs_0_.1), channel_id=1, source_target_pairs={{0,5},{1,4},{2,7},{3,6},{4,1},{5,0},{6,3},{7,2},{8,13},{9,12},{10,... | collective-permute-start | bytes 884744 | tf_op jit(solution)/shard_map/ppermute | solution.py:311
  3.9 13.5 %collective-permute-start.1 = (f32[96,768]{1,0:T(8,128)}, f32[96,768]{1,0:T(8,128)S(1)}, u32[]{:S(2)}, u32[]{:S(2)}) collective-permute-start(f32[96,768]{1,0:T(8,128)} %refs_0_.1), channel_id=1, source_target_pairs={{0,1},{1,0},{2,3},{3,2},{4,5},{5,4},{6,7},{7,6},{8,9},{9,8},{10,11... | collective-permute-start | bytes 884744 | tf_op jit(solution)/shard_map/ppermute | solution.py:311
  4.4 13.3 %collective-permute-start = (f32[96,768]{1,0:T(8,128)}, f32[96,768]{1,0:T(8,128)S(1)}, u32[]{:S(2)}, u32[]{:S(2)}) collective-permute-start(f32[96,768]{1,0:T(8,128)} %refs_0_.1), channel_id=1, source_target_pairs={{0,4},{1,5},{2,6},{3,7},{4,0},{5,1},{6,2},{7,3},{8,12},{9,13},{10,... | collective-permute-start | bytes 884744 | tf_op jit(solution)/shard_map/ppermute | solution.py:311
  4.5 27.3 %collective-permute-start.3 = (f32[96,768]{1,0:T(8,128)}, f32[96,768]{1,0:T(8,128)S(1)}, u32[]{:S(2)}, u32[]{:S(2)}) collective-permute-start(f32[96,768]{1,0:T(8,128)} %refs_0_.1), channel_id=1, source_target_pairs={{0,2},{1,3},{2,0},{3,1},{4,6},{5,7},{6,4},{7,5},{8,10},{9,11},{10,... | collective-permute-start | bytes 884744 | tf_op jit(solution)/shard_map/ppermute | solution.py:311
  12.0 27.6 %collective-permute-start.6 = (f32[96,768]{1,0:T(8,128)S(1)}, f32[96,768]{1,0:T(8,128)S(1)}, u32[]{:S(2)}, u32[]{:S(2)}) collective-permute-start(f32[96,768]{1,0:T(8,128)S(1)} %collective-permute-done.2.refs_3_), channel_id=1, source_target_pairs={{0,2},{1,3},{2,0},{3,1},{4,6},{5,7},{6,4},{7,5},{8,10},{9,11},{10,... | collective-permute-start | bytes 884744 | tf_op jit(solution)/shard_map/ppermute | solution.py:311
  17.5 23.9 %collective-permute-start.5 = (f32[96,768]{1,0:T(8,128)S(1)}, f32[96,768]{1,0:T(8,128)S(1)}, u32[]{:S(2)}, u32[]{:S(2)}) collective-permute-start(f32[96,768]{1,0:T(8,128)S(1)} %collective-permute-done.1.refs_2_), channel_id=1, source_target_pairs={{0,2},{1,3},{2,0},{3,1},{4,6},{5,7},{6,4},{7,5},{8,10},{9,11},{10,... | collective-permute-start | bytes 884744 | tf_op jit(solution)/shard_map/ppermute | solution.py:311
  17.8 24.9 %collective-permute-start.4 = (f32[96,768]{1,0:T(8,128)S(1)}, f32[96,768]{1,0:T(8,128)S(1)}, u32[]{:S(2)}, u32[]{:S(2)}) collective-permute-start(f32[96,768]{1,0:T(8,128)S(1)} %collective-permute-done.refs_1_), channel_id=1, source_target_pairs={{0,2},{1,3},{2,0},{3,1},{4,6},{5,7},{6,4},{7,5},{8,10},{9,11},{10,... | collective-permute-start | bytes 884744 | tf_op jit(solution)/shard_map/ppermute | solution.py:311
  29.2 23.2 %collective-permute-start.14 = (f32[392,128]{1,0:T(8,128)}, f32[392,128]{1,0:T(8,128)S(1)}, u32[]{:S(2)}, u32[]{:S(2)}) collective-permute-start(f32[392,128]{1,0:T(8,128)} %get-tuple-element.47), channel_id=1, source_target_pairs={{0,16},{8,24},{16,0},{24,8},{1,17},{9,25},{17,1},{25,9},{2,18},{10... | collective-permute-start | bytes 602120 | tf_op jit(solution)/shard_map/ppermute | solution.py:360
  31.8 20.6 %collective-permute-start.15 = (f32[392,128]{1,0:T(8,128)}, f32[392,128]{1,0:T(8,128)S(1)}, u32[]{:S(2)}, u32[]{:S(2)}) collective-permute-start(f32[392,128]{1,0:T(8,128)} %get-tuple-element.48), channel_id=1, source_target_pairs={{0,24},{8,16},{16,8},{24,0},{1,25},{9,17},{17,9},{25,1},{2,26},{10... | collective-permute-start | bytes 602120 | tf_op jit(solution)/shard_map/ppermute | solution.py:360
  39.6 28.1 %collective-permute-start.20 = (f32[392,128]{1,0:T(8,128)}, f32[392,128]{1,0:T(8,128)S(1)}, u32[]{:S(2)}, u32[]{:S(2)}) collective-permute-start(f32[392,128]{1,0:T(8,128)} %first.1), channel_id=1, source_target_pairs={{0,16},{8,24},{16,0},{24,8},{1,17},{9,25},{17,1},{25,9},{2,18},{10... | collective-permute-start | bytes 602120 | tf_op jit(solution)/shard_map/ppermute | solution.py:360
  41.3 28.9 %collective-permute-start.19 = (f32[392,128]{1,0:T(8,128)}, f32[392,128]{1,0:T(8,128)}, u32[]{:S(2)}, u32[]{:S(2)}) collective-permute-start(f32[392,128]{1,0:T(8,128)} %get-tuple-element.54), channel_id=1, source_target_pairs={{0,8},{8,0},{16,24},{24,16},{1,9},{9,1},{17,25},{25,17},{2,10},{10... | collective-permute-start | bytes 602120 | tf_op jit(solution)/shard_map/ppermute | solution.py:360
  42.7 27.5 %collective-permute-start.21 = (f32[392,128]{1,0:T(8,128)}, f32[392,128]{1,0:T(8,128)}, u32[]{:S(2)}, u32[]{:S(2)}) collective-permute-start(f32[392,128]{1,0:T(8,128)} %get-tuple-element.55), channel_id=1, source_target_pairs={{0,24},{8,16},{16,8},{24,0},{1,25},{9,17},{17,9},{25,1},{2,26},{10... | collective-permute-start | bytes 602120 | tf_op jit(solution)/shard_map/ppermute | solution.py:360
  52.4 35.2 %collective-permute-start.7 = (f32[392,128]{1,0:T(8,128)}, f32[392,128]{1,0:T(8,128)S(1)}, u32[]{:S(2)}, u32[]{:S(2)}) collective-permute-start(f32[392,128]{1,0:T(8,128)} %get-tuple-element.39), channel_id=1, source_target_pairs={{0,8},{8,0},{16,24},{24,16},{1,9},{9,1},{17,25},{25,17},{2,10},{10... | collective-permute-start | bytes 602120 | tf_op jit(solution)/shard_map/ppermute | solution.py:360
  52.4 38.6 %collective-permute-start.8 = (f32[392,128]{1,0:T(8,128)}, f32[392,128]{1,0:T(8,128)S(1)}, u32[]{:S(2)}, u32[]{:S(2)}) collective-permute-start(f32[392,128]{1,0:T(8,128)} %get-tuple-element.40), channel_id=1, source_target_pairs={{0,16},{8,24},{16,0},{24,8},{1,17},{9,25},{17,1},{25,9},{2,18},{10... | collective-permute-start | bytes 602120 | tf_op jit(solution)/shard_map/ppermute | solution.py:360
  67.7 23.3 %collective-permute-start.9 = (f32[392,128]{1,0:T(8,128)S(1)}, f32[392,128]{1,0:T(8,128)S(1)}, u32[]{:S(2)}, u32[]{:S(2)}) collective-permute-start(f32[392,128]{1,0:T(8,128)S(1)} %copy-done.7), channel_id=1, source_target_pairs={{0,24},{8,16},{16,8},{24,0},{1,25},{9,17},{17,9},{25,1},{2,26},{10... | collective-permute-start | bytes 602120 | tf_op jit(solution)/shard_map/ppermute | solution.py:360
  70.2 36.3 %collective-permute-start.16 = (f32[392,128]{1,0:T(8,128)S(1)}, f32[392,128]{1,0:T(8,128)S(1)}, u32[]{:S(2)}, u32[]{:S(2)}) collective-permute-start(f32[392,128]{1,0:T(8,128)S(1)} %get-tuple-element.50), channel_id=1, source_target_pairs={{0,16},{8,24},{16,0},{24,8},{1,17},{9,25},{17,1},{25,9},{2,18},{10... | collective-permute-start | bytes 602120 | tf_op jit(solution)/shard_map/ppermute | solution.py:360
  75.3 35.8 %collective-permute-start.22 = (f32[392,128]{1,0:T(8,128)S(1)}, f32[392,128]{1,0:T(8,128)S(1)}, u32[]{:S(2)}, u32[]{:S(2)}) collective-permute-start(f32[392,128]{1,0:T(8,128)S(1)} %get-tuple-element.57), channel_id=1, source_target_pairs={{0,16},{8,24},{16,0},{24,8},{1,17},{9,25},{17,1},{25,9},{2,18},{10... | collective-permute-start | bytes 602120 | tf_op jit(solution)/shard_map/ppermute | solution.py:360
  87.6 26.6 %collective-permute-start.23 = (f32[392,128]{1,0:T(8,128)S(1)}, f32[392,128]{1,0:T(8,128)S(1)}, u32[]{:S(2)}, u32[]{:S(2)}) collective-permute-start(f32[392,128]{1,0:T(8,128)S(1)} %get-tuple-element.58), channel_id=1, source_target_pairs={{0,24},{8,16},{16,8},{24,0},{1,25},{9,17},{17,9},{25,1},{2,26},{10... | collective-permute-start | bytes 602120 | tf_op jit(solution)/shard_map/ppermute | solution.py:360
  91.0 28.2 %collective-permute-start.24 = (f32[392,128]{1,0:T(8,128)S(1)}, f32[392,128]{1,0:T(8,128)S(1)}, u32[]{:S(2)}, u32[]{:S(2)}) collective-permute-start(f32[392,128]{1,0:T(8,128)S(1)} %get-tuple-element.59), channel_id=1, source_target_pairs={{0,8},{8,0},{16,24},{24,16},{1,9},{9,1},{17,25},{25,17},{2,10},{10... | collective-permute-start | bytes 602120 | tf_op jit(solution)/shard_map/ppermute | solution.py:360
  91.0 31.4 %collective-permute-start.17 = (f32[392,128]{1,0:T(8,128)S(1)}, f32[392,128]{1,0:T(8,128)S(1)}, u32[]{:S(2)}, u32[]{:S(2)}) collective-permute-start(f32[392,128]{1,0:T(8,128)S(1)} %get-tuple-element.51), channel_id=1, source_target_pairs={{0,24},{8,16},{16,8},{24,0},{1,25},{9,17},{17,9},{25,1},{2,26},{10... | collective-permute-start | bytes 602120 | tf_op jit(solution)/shard_map/ppermute | solution.py:360
  106.5 16.0 %collective-permute-start.18 = (f32[392,128]{1,0:T(8,128)S(1)}, f32[392,128]{1,0:T(8,128)S(1)}, u32[]{:S(2)}, u32[]{:S(2)}) collective-permute-start(f32[392,128]{1,0:T(8,128)S(1)} %get-tuple-element.52), channel_id=1, source_target_pairs={{0,8},{8,0},{16,24},{24,16},{1,9},{9,1},{17,25},{25,17},{2,10},{10... | collective-permute-start | bytes 602120 | tf_op jit(solution)/shard_map/ppermute | solution.py:360
  111.1 21.1 %collective-permute-start.12 = (f32[392,128]{1,0:T(8,128)S(1)}, f32[392,128]{1,0:T(8,128)S(1)}, u32[]{:S(2)}, u32[]{:S(2)}) collective-permute-start(f32[392,128]{1,0:T(8,128)S(1)} %get-tuple-element.44), channel_id=1, source_target_pairs={{0,16},{8,24},{16,0},{24,8},{1,17},{9,25},{17,1},{25,9},{2,18},{10... | collective-permute-start | bytes 602120 | tf_op jit(solution)/shard_map/ppermute | solution.py:360
  114.2 19.0 %collective-permute-start.11 = (f32[392,128]{1,0:T(8,128)S(1)}, f32[392,128]{1,0:T(8,128)S(1)}, u32[]{:S(2)}, u32[]{:S(2)}) collective-permute-start(f32[392,128]{1,0:T(8,128)S(1)} %get-tuple-element.43), channel_id=1, source_target_pairs={{0,8},{8,0},{16,24},{24,16},{1,9},{9,1},{17,25},{25,17},{2,10},{10... | collective-permute-start | bytes 602120 | tf_op jit(solution)/shard_map/ppermute | solution.py:360
  119.2 14.9 %collective-permute-start.10 = (f32[392,128]{1,0:T(8,128)S(1)}, f32[392,128]{1,0:T(8,128)S(1)}, u32[]{:S(2)}, u32[]{:S(2)}) collective-permute-start(f32[392,128]{1,0:T(8,128)S(1)} %get-tuple-element.42), channel_id=1, source_target_pairs={{0,24},{8,16},{16,8},{24,0},{1,25},{9,17},{17,9},{25,1},{2,26},{10... | collective-permute-start | bytes 602120 | tf_op jit(solution)/shard_map/ppermute | solution.py:360
  (11 other events, 344.8 us)
